TPU v7x, 128 devices: a whole 4x4x4 slice. The times are simulated.
128 devices in a mesh: dp: 8 (over x, z_lo), space: 16 (over z_hi, y, core).
Axes of the slice: x: 4, y: 4, z: 4 (z_hi: 2, z_lo: 2; z = z_hi * 2 + z_lo), core: 2. Of those that a mesh axis runs over, the one named last changes fastest.
Arguments:
- latent: bfloat16 [8, 64, 512, 320], P('dp', 'space'), may hold values from -40 to 40
- timesteps: int32 [8], P('dp'), may hold values from 0 to 999
- norm_gain: float32 [320], replicated, may hold values from 0.1 to 1.9
- norm_bias: float32 [320], replicated, may hold values from -3 to 3
- conv_weight: bfloat16 [3, 3, 320, 320], replicated, may hold values from -0.109375 to 0.109375
- conv_bias: float32 [320], replicated, may hold values from -3 to 3
- time_weight: bfloat16 [320, 320], replicated, may hold values from -0.5 to 0.5
- cotangent: bfloat16 [8, 64, 512, 320], P('dp', 'space'), may hold values from -40 to 40
Outputs:
- block_out: bfloat16 [8, 64, 512, 320], P('dp', 'space')
- latent_grad: bfloat16 [8, 64, 512, 320], P('dp', 'space')
- weight_grad: float32 [3, 3, 320, 320], replicated
- time_grad: float32 [320, 320], replicated
All inputs are finite; a program needn't handle non-finite values.
Results may differ from a plain program's by a relative error of at most 0.001.
The roundings to bfloat16 on the way count: a program that leaves them out, or rounds other values in their place, can miss the bound.
Values may be sent and summed in bfloat16 or wider, within the bound.
A program may use at most 128 MiB of HBM per device.

v0:
```python
import math

import jax
import jax.numpy as jnp
from jax import lax
from jax.sharding import PartitionSpec as P

GROUPS = 32


epsilon = 1e-05


def sent_to_all(value, axis):
    count = lax.axis_size(axis)
    return lax.all_to_all(
        jnp.broadcast_to(value[None], (count, *value.shape)), axis, 0, 0, tiled=True
    )


def taken_together(value, axis):
    everything = sent_to_all(value, axis)
    return jnp.sum(everything, axis=0)


def padded(cells, sides, width):
    for axis, dim in sides:
        count = lax.axis_size(axis)
        ends = count - 1
        head = lax.slice_in_dim(cells, 0, width, axis=dim)
        tail = lax.slice_in_dim(cells, cells.shape[dim] - width, cells.shape[dim], axis=dim)
        cells = jnp.concatenate(
            [
                lax.ppermute(tail, axis, [(i, (i + 1) % count) for i in range(ends)]),
                cells,
                lax.ppermute(head, axis, [((i + 1) % count, i) for i in range(ends)]),
            ],
            axis=dim,
        )
    return cells


def packed_total(arrays, axis):
    flat, at, done = (jnp.concatenate([a.reshape(-1) for a in arrays]), 0, [])
    so_far = taken_together(flat, axis)
    for a in arrays:
        done.append(so_far[at : at + a.size].reshape(a.shape))
        at += a.size
    return tuple(done)


def per_device(
    latent, timesteps, norm_gain, norm_bias, conv_weight, conv_bias, time_weight, cotangent
):
    images, row_count, col_count, channels = latent.shape
    per_group = channels // GROUPS
    local_cells = row_count * col_count * per_group
    total_cells = local_cells * lax.axis_size("space")
    latent_wide = latent.astype(jnp.float32).reshape(
        images, row_count * col_count, GROUPS, per_group
    )
    group_mean = taken_together(jnp.sum(latent_wide, axis=(1, 3)), "space") / total_cells
    centered = latent_wide - group_mean[:, None, :, None]
    group_var = taken_together(jnp.sum(centered * centered, axis=(1, 3)), "space") / total_cells
    inverse_std = lax.rsqrt(group_var + epsilon)
    normed = (latent_wide - group_mean[:, None, :, None]) * inverse_std[:, None, :, None]
    normed = normed.reshape(images, row_count, col_count, channels)
    shifted = normed * norm_gain + norm_bias
    sigmoid_act = jax.nn.sigmoid(shifted)
    activated = (shifted * sigmoid_act).astype(jnp.bfloat16)
    padded_act = padded(activated, (("space", 1),), 1)
    padded_act = jnp.pad(padded_act, ((0, 0), (0, 0), (1, 1), (0, 0)))
    padded_grad = padded(cotangent, (("space", 1),), 1)
    padded_grad = jnp.pad(padded_grad, ((0, 0), (0, 0), (1, 1), (0, 0)))
    grad_flat = cotangent.reshape(-1, channels)
    conv_out = jnp.zeros((images * row_count * col_count, channels), jnp.float32)
    act_grad = jnp.zeros((images * row_count * col_count, channels), jnp.float32)
    weight_rows = []
    for tap_row in range(3):
        weight_cols = []
        for tap_col in range(3):
            piece = padded_act[
                :, tap_row : tap_row + row_count, tap_col : tap_col + col_count
            ].reshape(-1, channels)
            conv_out = conv_out + jnp.dot(
                piece, conv_weight[tap_row, tap_col], preferred_element_type=jnp.float32
            )
            grad_piece = padded_grad[
                :, 2 - tap_row : 2 - tap_row + row_count, 2 - tap_col : 2 - tap_col + col_count
            ].reshape(-1, channels)
            act_grad = act_grad + jnp.dot(
                grad_piece, conv_weight[tap_row, tap_col].T, preferred_element_type=jnp.float32
            )
            weight_cols.append(jnp.dot(piece.T, grad_flat, preferred_element_type=jnp.float32))
        weight_rows.append(jnp.stack(weight_cols))
    weight_part = jnp.stack(weight_rows)
    half_count = channels // 2
    frequency = jnp.exp(-math.log(10000.0) * jnp.arange(half_count, dtype=jnp.float32) / half_count)
    angles = timesteps.astype(jnp.float32)[:, None] * frequency[None, :]
    embedding = jnp.concatenate([jnp.cos(angles), jnp.sin(angles)], axis=1).astype(jnp.bfloat16)
    time_bias = jnp.dot(embedding, time_weight, preferred_element_type=jnp.float32)
    block_out = (
        latent.astype(jnp.float32)
        + conv_out.reshape(images, row_count, col_count, channels)
        + conv_bias
        + time_bias[:, None, None, :]
    )
    block_out = block_out.astype(jnp.bfloat16)
    act_grad = act_grad.reshape(images, row_count, col_count, channels)
    normed_grad = act_grad * sigmoid_act * (1.0 + shifted * (1.0 - sigmoid_act)) * norm_gain
    grouped_grad = normed_grad.reshape(images, row_count * col_count, GROUPS, per_group)
    grouped_norm = normed.reshape(images, row_count * col_count, GROUPS, per_group)
    first_sum, second_sum = packed_total(
        (jnp.sum(grouped_grad, axis=(1, 3)), jnp.sum(grouped_grad * grouped_norm, axis=(1, 3))),
        "space",
    )
    first_mean = first_sum / total_cells
    second_mean = second_sum / total_cells
    change = inverse_std[:, None, :, None] * (
        grouped_grad - first_mean[:, None, :, None] - grouped_norm * second_mean[:, None, :, None]
    )
    latent_grad = (
        cotangent.astype(jnp.float32) + change.reshape(images, row_count, col_count, channels)
    ).astype(jnp.bfloat16)
    grad_total = jnp.sum(cotangent.astype(jnp.float32), axis=(1, 2))
    time_part = jnp.einsum(
        "nk,no->ko", embedding.astype(jnp.float32), grad_total, precision=lax.Precision.HIGHEST
    )
    weight_grad, time_grad = lax.psum((weight_part, time_part), ("dp", "space"))
    return (block_out, latent_grad, weight_grad, time_grad)


def solution(mesh):
    return jax.shard_map(
        per_device,
        mesh=mesh,
        in_specs=(
            P("dp", "space", None, None),
            P("dp"),
            P(),
            P(),
            P(),
            P(),
            P(),
            P("dp", "space", None, None),
        ),
        out_specs=(P("dp", "space", None, None), P("dp", "space", None, None), P(), P()),
        check_vma=False,
    )
```

profile of v0, /device:TPU:1, one launch (start us, length us, event | category | flops | bytes accessed | tf_op | source)
XLA Modules:
  0.0 323.2 jit_solution(9966468453335314752)
XLA Ops:
  7.2 1.7 convert_reduce_fusion
  9.8 9.3 %all-to-all-start = ((f32[16,1,32]{2,1,0:T(1,128)}), f32[16,1,32]{2,1,0:T(1,128)S(1)}, u32[]{:S(2)}, u32[]{:S(2)}) async-start(f32[16,1,32]{2,1,0:T(1,128)} %broadcast_in_dim.6), calls=%async_computation | async-start | bytes 16384 | tf_op jit(solution)/shard_map/all_to_all | solution.py:16
  19.9 2.0 collective-permute-start.3
  22.0 3.5 %collective-permute-start.2 = (bf16[1,1,512,320]{2,3,1,0:T(8,128)(2,1)}, bf16[1,1,512,320]{2,3,1,0:T(8,128)(2,1)S(1)}, u32[]{:S(2)}, u32[]{:S(2)}) collective-permute-start(bf16[1,1,512,320]{2,3,1,0:T(8,128)(2,1)} %get-tuple-element.27), channel_id=1, source_target_pairs={{0,1},{1,2},{2,3},{3,4},{4,5},{5,6},{6,7},{7,8},{8,9},{9,10},{10,1... | collective-permute-start | bytes 983048 | tf_op jit(solution)/shard_map/ppermute | solution.py:34
  27.9 7.9 %all-to-all-start.1 = ((f32[16,1,32]{2,1,0:T(1,128)}), f32[16,1,32]{2,1,0:T(1,128)S(1)}, u32[]{:S(2)}, u32[]{:S(2)}) async-start(f32[16,1,32]{2,1,0:T(1,128)} %broadcast_in_dim.7), calls=%async_computation.1 | async-start | bytes 16384 | tf_op jit(solution)/shard_map/all_to_all | solution.py:16
  35.9 1.0 copy.70
  37.3 5.4 %all-to-all-done.1 = f32[16,1,32]{2,1,0:T(1,128)S(1)} async-done(((f32[16,1,32]{2,1,0:T(1,128)}), f32[16,1,32]{2,1,0:T(1,128)S(1)}, u32[]{:S(2)}, u32[]{:S(2)}) %all-to-all-start.1) | async-done | bytes 2080 | tf_op jit(solution)/shard_map/all_to_all | solution.py:16
  42.9 1.7 select_maximum_fusion
  44.6 2.6 fusion.145
  47.3 1.0 copy.66
  48.9 1.0 copy.67
  50.3 1.0 copy.68
  51.7 1.0 copy.69
  53.0 1.0 copy.71
  54.4 1.0 copy.72
  55.8 1.0 copy.73
  57.2 1.0 copy.74
  58.6 1.3 copy-done.5
  59.8 1.0 fusion.114
  66.8 2.3 convolution_add_fusion
  69.2 4.6 %reshape.279 = f32[1,4,512,320]{2,1,3,0:T(4,128)} reshape(f32[2048,320]{0,1:T(8,128)} %convolution_add_fusion) | data formatting | bytes 5242880 | tf_op jit(solution)/shard_map/reshape | solution.py:109
  73.8 5.0 %fusion.143 = (f32[320]{0:T(512)S(1)}, f32[320]{0:T(512)S(1)}, f32[1,4,512,320]{2,3,1,0:T(8,128)}, bf16[1,4,512,320]{2,3,1,0:T(8,128)(2,1)S(1)}) fusion(f32[320]{0:T(512)S(1)} %mul.119, f32[320]{0:T(512)S(1)} %sub.54, bf16[1,4,512,320]{2,3,1,0:T(8,128)(2,1)} %param.8, f32[320]{0:T(512)S(1)} %copy-done.18, f32[320]{0:T(512)S(1)} %copy-done.19, ...), kind=kLoop, calls=%fused_computation.154 | loop fusion | flops 12451200 | bytes 7872000 | tf_op jit(solution)/shard_map/reduce_sum | solution.py:114
  79.9 3.9 %all-to-all-start.2 = ((f32[16,1,64]{2,1,0:T(1,128)}), f32[16,1,64]{2,1,0:T(1,128)S(1)}, u32[]{:S(2)}, u32[]{:S(2)}) async-start(f32[16,1,64]{2,1,0:T(1,128)} %broadcast_in_dim.8), calls=%async_computation.2 | async-start | bytes 16384 | tf_op jit(solution)/shard_map/all_to_all | solution.py:16
  84.7 2.1 collective-permute-start.1
  86.8 3.4 %collective-permute-start = (bf16[1,1,512,320]{2,3,1,0:T(8,128)(2,1)}, bf16[1,1,512,320]{2,3,1,0:T(8,128)(2,1)S(1)}, u32[]{:S(2)}, u32[]{:S(2)}) collective-permute-start(bf16[1,1,512,320]{2,3,1,0:T(8,128)(2,1)} %get-tuple-element.31), channel_id=1, source_target_pairs={{0,1},{1,2},{2,3},{3,4},{4,5},{5,6},{6,7},{7,8},{8,9},{9,10},{10,1... | collective-permute-start | bytes 983048 | tf_op jit(solution)/shard_map/ppermute | solution.py:34
  90.2 1.7 fusion.73
  92.9 1.4 copy.81
  94.8 1.7 select_maximum_fusion.2
  96.5 2.3 fusion.146
  98.9 1.7 fusion.93
  101.8 1.6 fusion.88
  103.4 1.7 fusion.83
  107.0 1.6 fusion.58
  108.7 1.7 fusion.53
  110.3 1.7 fusion.78
  112.0 1.6 fusion.68
  115.1 1.3 copy-done.6
  117.6 1.0 copy.58
  119.0 1.0 copy.59
  120.7 1.0 copy.61
  122.1 1.0 copy.62
  123.9 1.0 copy.64
  132.0 2.4 convolution_add_fusion.8
  134.4 4.8 %reshape.269 = f32[1,4,512,320]{2,1,3,0:T(4,128)} reshape(f32[2048,320]{0,1:T(8,128)} %convolution_add_fusion.8) | data formatting | bytes 5242880 | tf_op jit(solution)/shard_map/reshape | solution.py:104
  139.2 5.8 %convert_reduce_fusion.1 = (f32[320]{0:T(512)S(1)}, bf16[1,4,512,320]{2,3,1,0:T(8,128)(2,1)}, bf16[1,4,512,320]{2,3,1,0:T(8,128)(2,1)}) fusion(bf16[1,4,512,320]{2,3,1,0:T(8,128)(2,1)S(1)} %copy-done.2, f32[320]{0:T(512)S(1)} %mul.134, f32[320]{0:T(512)S(1)} %sub.54, bf16[1,4,512,320]{2,3,1,0:T(8,128)(2,1)S(1)} %copy-done.4, ...), kind=kLoop, calls=%fused_computation.7 | loop fusion | flops 9830080 | bytes 10494720 | tf_op jit(solution)/shard_map/reduce_sum | solution.py:125
  147.7 2.4 pad_maximum_fusion
  150.1 160.6 %all-reduce.5.cloned.1.call-done = (f32[3,3,320,320]{3,2,1,0:T(8,128)}, f32[320,320]{1,0:T(8,128)}) async-done(((f32[3,3,320,320]{3,2,1,0:T(8,128)}, f32[320,320]{1,0:T(8,128)}), (f32[3,3,320,320]{3,2,1,0:T(8,128)}, f32[320,320]{1,0:T(8,128)})) %all-reduce.5.cloned.1.call-update) | async-done | bytes 4096016 | tf_op jit(solution)/shard_map/psum | solution.py:129
  310.7 4.7 %copy.103 = f32[3,3,320,320]{3,2,1,0:T(8,128)} copy(f32[3,3,320,320]{3,2,1,0:T(8,128)} %get-tuple-element.43) | data formatting | bytes 7372800
  (122 shorter events, 35.1 us)
Async XLA Ops:
  7.2 28.6 %copy-start = (bf16[320,320]{1,0:T(8,128)(2,1)S(1)}, bf16[320,320]{1,0:T(8,128)(2,1)}, u32[]{:S(2)}) copy-start(bf16[320,320]{1,0:T(8,128)(2,1)} %param.14) | copy-start | bytes 614404
  7.2 11.9 %copy-start.2 = (bf16[1,4,512,320]{2,3,1,0:T(8,128)(2,1)S(1)}, bf16[1,4,512,320]{2,3,1,0:T(8,128)(2,1)}, u32[]{:S(2)}) copy-start(bf16[1,4,512,320]{2,3,1,0:T(8,128)(2,1)} %param.15) | copy-start | bytes 3932164
  7.2 19.3 %copy-start.3 = (bf16[1,4,512,320]{2,3,1,0:T(8,128)(2,1)S(1)}, bf16[1,4,512,320]{2,3,1,0:T(8,128)(2,1)}, u32[]{:S(2)}) copy-start(bf16[1,4,512,320]{2,3,1,0:T(8,128)(2,1)} %param.8) | copy-start | bytes 3932164
  9.8 16.5 %all-to-all-start = ((f32[16,1,32]{2,1,0:T(1,128)}), f32[16,1,32]{2,1,0:T(1,128)S(1)}, u32[]{:S(2)}, u32[]{:S(2)}) async-start(f32[16,1,32]{2,1,0:T(1,128)} %broadcast_in_dim.6), calls=%async_computation | async-start | bytes 16384 | tf_op jit(solution)/shard_map/all_to_all | solution.py:16
  19.9 23.0 %collective-permute-start.3 = (bf16[1,1,512,320]{2,3,1,0:T(8,128)(2,1)}, bf16[1,1,512,320]{2,3,1,0:T(8,128)(2,1)S(1)}, u32[]{:S(2)}, u32[]{:S(2)}) collective-permute-start(bf16[1,1,512,320]{2,3,1,0:T(8,128)(2,1)} %get-tuple-element.28), channel_id=1, source_target_pairs={{1,0},{2,1},{3,2},{4,3},{5,4},{6,5},{7,6},{8,7},{9,8},{10,9},{11,1... | collective-permute-start | bytes 983048 | tf_op jit(solution)/shard_map/ppermute | solution.py:36
  22.0 21.0 %collective-permute-start.2 = (bf16[1,1,512,320]{2,3,1,0:T(8,128)(2,1)}, bf16[1,1,512,320]{2,3,1,0:T(8,128)(2,1)S(1)}, u32[]{:S(2)}, u32[]{:S(2)}) collective-permute-start(bf16[1,1,512,320]{2,3,1,0:T(8,128)(2,1)} %get-tuple-element.27), channel_id=1, source_target_pairs={{0,1},{1,2},{2,3},{3,4},{4,5},{5,6},{6,7},{7,8},{8,9},{9,10},{10,1... | collective-permute-start | bytes 983048 | tf_op jit(solution)/shard_map/ppermute | solution.py:34
  27.9 14.8 %all-to-all-start.1 = ((f32[16,1,32]{2,1,0:T(1,128)}), f32[16,1,32]{2,1,0:T(1,128)S(1)}, u32[]{:S(2)}, u32[]{:S(2)}) async-start(f32[16,1,32]{2,1,0:T(1,128)} %broadcast_in_dim.7), calls=%async_computation.1 | async-start | bytes 16384 | tf_op jit(solution)/shard_map/all_to_all | solution.py:16
  58.2 1.6 copy-start.5
  69.2 4.6 %copy-start.18 = (f32[320]{0:T(512)S(1)}, f32[320]{0:T(512)}, u32[]{:S(2)}) copy-start(f32[320]{0:T(512)} %param.11) | copy-start | bytes 3844
  69.2 4.6 %copy-start.19 = (f32[320]{0:T(512)S(1)}, f32[320]{0:T(512)}, u32[]{:S(2)}) copy-start(f32[320]{0:T(512)} %param.10) | copy-start | bytes 3844
  79.9 14.5 %all-to-all-start.2 = ((f32[16,1,64]{2,1,0:T(1,128)}), f32[16,1,64]{2,1,0:T(1,128)S(1)}, u32[]{:S(2)}, u32[]{:S(2)}) async-start(f32[16,1,64]{2,1,0:T(1,128)} %broadcast_in_dim.8), calls=%async_computation.2 | async-start | bytes 16384 | tf_op jit(solution)/shard_map/all_to_all | solution.py:16
  83.8 227.0 %all-reduce.5.cloned.1.call-start = ((), (), s32[]{:S(2)}) async-start(), calls=%async_computation.3 | async-start | bytes 9830400 | tf_op jit(solution)/shard_map/psum | solution.py:129
  84.7 10.1 %collective-permute-start.1 = (bf16[1,1,512,320]{2,3,1,0:T(8,128)(2,1)}, bf16[1,1,512,320]{2,3,1,0:T(8,128)(2,1)S(1)}, u32[]{:S(2)}, u32[]{:S(2)}) collective-permute-start(bf16[1,1,512,320]{2,3,1,0:T(8,128)(2,1)} %get-tuple-element.32), channel_id=1, source_target_pairs={{1,0},{2,1},{3,2},{4,3},{5,4},{6,5},{7,6},{8,7},{9,8},{10,9},{11,1... | collective-permute-start | bytes 983048 | tf_op jit(solution)/shard_map/ppermute | solution.py:36
  86.8 8.0 %collective-permute-start = (bf16[1,1,512,320]{2,3,1,0:T(8,128)(2,1)}, bf16[1,1,512,320]{2,3,1,0:T(8,128)(2,1)S(1)}, u32[]{:S(2)}, u32[]{:S(2)}) collective-permute-start(bf16[1,1,512,320]{2,3,1,0:T(8,128)(2,1)} %get-tuple-element.31), channel_id=1, source_target_pairs={{0,1},{1,2},{2,3},{3,4},{4,5},{5,6},{6,7},{7,8},{8,9},{9,10},{10,1... | collective-permute-start | bytes 983048 | tf_op jit(solution)/shard_map/ppermute | solution.py:34
  114.7 1.6 copy-start.6
  127.1 1.3 copy-start.7
  134.4 4.8 %copy-start.4 = (bf16[1,4,512,320]{2,3,1,0:T(8,128)(2,1)S(1)}, bf16[1,4,512,320]{2,3,1,0:T(8,128)(2,1)}, u32[]{:S(2)}) copy-start(bf16[1,4,512,320]{2,3,1,0:T(8,128)(2,1)} %param.8) | copy-start | bytes 3932164
  134.4 4.8 %copy-start.17 = (f32[320]{0:T(512)S(1)}, f32[320]{0:T(512)}, u32[]{:S(2)}) copy-start(f32[320]{0:T(512)} %param.13) | copy-start | bytes 3844
  139.2 6.7 %copy-start.9 = (f32[1,320,320]{2,1,0:T(8,128)S(1)}, f32[1,320,320]{2,1,0:T(8,128)}, u32[]{:S(2)}) copy-start(f32[1,320,320]{2,1,0:T(8,128)} %fusion.93) | copy-start | bytes 1228804
  139.2 6.7 %copy-start.11 = (f32[1,320,320]{2,1,0:T(8,128)S(1)}, f32[1,320,320]{2,1,0:T(8,128)}, u32[]{:S(2)}) copy-start(f32[1,320,320]{2,1,0:T(8,128)} %fusion.88) | copy-start | bytes 1228804
  139.2 6.7 %copy-start.15 = (f32[1,320,320]{2,1,0:T(8,128)S(1)}, f32[1,320,320]{2,1,0:T(8,128)}, u32[]{:S(2)}) copy-start(f32[1,320,320]{2,1,0:T(8,128)} %fusion.83) | copy-start | bytes 1228804
  145.9 1.0 copy-start.8
  145.9 1.2 copy-start.10
  145.9 1.3 copy-start.12
  145.9 1.5 copy-start.13
  145.9 1.6 copy-start.14
  310.7 4.7 %copy-start.16 = (f32[320,320]{1,0:T(8,128)S(1)}, f32[320,320]{1,0:T(8,128)}, u32[]{:S(2)}) copy-start(f32[320,320]{1,0:T(8,128)} %get-tuple-element.44) | copy-start | bytes 1228804
  310.7 5.5 %copy-start.1 = (bf16[320,320]{1,0:T(8,128)(2,1)S(1)}, bf16[320,320]{1,0:T(8,128)(2,1)}, u32[]{:S(2)}) copy-start(bf16[320,320]{1,0:T(8,128)(2,1)} %param.14) | copy-start | bytes 614404
Sparse Core Ops, SparseCore 0:
  150.3 160.4 all-reduce.4
where the time goes:
time: 328 us; the launch traced here: 323 us
  waiting for transfers between devices  166 us (51%)
  local copies, waits for them, and re-layouts  55.1 us (17%)
  matrix products  33.1 us (10%)
  starting transfers between devices  32.1 us (10%)
  other arithmetic  21.3 us (6%)
  between operations  15.5 us (5%)
    psum x1, waiting for transfers between devices, per_device(): weight_grad, time_grad = lax.psum((weight_part, time_part), ('dp', 'space'))  161 us
    all_to_all x3, starting transfers between devices, sent_to_all(): lax.all_to_all(jnp.broadcast_to(value[None], (count, *value.shape)), axis...  21 us
    unnamed x61, local copies, waits for them, and re-layouts  18.8 us
    dot_general x9, matrix products, per_device(): jnp.dot(piece.T, grad_flat, preferred_element_type=jnp.float32)  14.2 us
    slice x9, local copies, waits for them, and re-layouts, per_device(): padded_grad[:, 2 - tap_row:2 - tap_row + row_count, 2 - tap_col:2 - tap_c...  10.8 us
    slice x9, local copies, waits for them, and re-layouts, per_device(): padded_act[:, tap_row:tap_row + row_count, tap_col:tap_col + col_count]  10.4 us
    dot_general x9, matrix products, per_device(): jnp.dot(piece, conv_weight[tap_row, tap_col], preferred_element_type=jnp....  9.51 us
    dot_general x9, matrix products, per_device(): jnp.dot(grad_piece, conv_weight[tap_row, tap_col].T, preferred_element_ty...  9.28 us
  transfers between devices with their start and end apart: 8, of which 2 were waited for; matrix products, arithmetic and copies ran while one was open for 3% of the time, Pallas kernels for 0%

commit v1 on v0

v1 whole, which is shorter than its diff:
```python
import math

import jax
import jax.numpy as jnp
from jax import lax
from jax.experimental import pallas as pl
from jax.experimental.pallas import tpu as pltpu
from jax.sharding import PartitionSpec as P

GROUPS = 32
EPSILON = 1e-05
CH = 320
ROWS = 4
COLS = 512
CELLS = ROWS * COLS
PER_GROUP = CH // GROUPS
SPACE = 16
DP = 8
TILE = 256
TILES = CELLS // TILE
MESH = pl.DeviceIdType.MESH
F32 = jnp.float32
BF16 = jnp.bfloat16

HALO = 0
STATS = 4
BACK = STATS + 15
TIME = BACK + 15
REDUCE = TIME + 7
PER_COLOUR = 17
REMOTE = REDUCE + 3 * PER_COLOUR


def device_at(x, y, z, core):
    return (x * 2 + lax.rem(z, 2), lax.div(z, 2) * 8 + y * 2 + core)


def kernel(
    emb_hbm, x_hbm, g_hbm, w_hbm, tw_hbm, gain_hbm, nbias_hbm, cbias_hbm,
    out_hbm, lg_hbm, wg_hbm, tg_hbm,
    xb, gb, wb, wt, tw, emb, gain, nbias, cbias,
    g3, a3, at, ng, mean_s, inv_s, outb, lgb, wgo, tgo,
    st_out, st_rx, bk_out, bk_rx, tm_out, tm_rx,
    wg, rx0, rx1, s1, rx2, s2, rx3, fin, res,
    bacc, local, send, recv,
):
    dp = lax.axis_index("dp")
    sp = lax.axis_index("space")
    x = lax.div(dp, 2)
    z = lax.div(sp, 8) * 2 + lax.rem(dp, 2)
    y = lax.rem(lax.div(sp, 2), 4)
    core = lax.rem(sp, 2)
    other = 1 - core
    place = {"x": x, "y": y, "z": z}

    def along(axis, d):
        spot = dict(place)
        spot[axis] = lax.rem(place[axis] + d, 4)
        return spot[axis], device_at(spot["x"], spot["y"], spot["z"], core)

    def space_peer(d):
        return (dp, lax.rem(sp + d, SPACE))

    def dp_peer(d):
        return (lax.rem(dp + d, DP), sp)

    partner = (dp, sp + 1 - 2 * core)

    def remote(number, src, dst, device):
        return pltpu.make_async_remote_copy(
            src_ref=src, dst_ref=dst, send_sem=send.at[number], recv_sem=recv.at[number],
            device_id=device, device_id_type=MESH,
        )

    def load(number, src, dst):
        return pltpu.make_async_copy(src, dst, local.at[number])

    loads = {
        "x": load(0, x_hbm, xb.at[pl.ds(COLS, CELLS)]),
        "g": load(1, g_hbm, gb.at[pl.ds(COLS, CELLS)]),
        "tw": load(2, tw_hbm, tw),
        "emb": load(3, emb_hbm, emb),
        "gain": load(4, gain_hbm, gain),
        "nbias": load(5, nbias_hbm, nbias),
        "cbias": load(6, cbias_hbm, cbias),
        "w0": load(7, w_hbm.at[0], wb.at[0, pl.ds(0, 960)]),
        "w1": load(8, w_hbm.at[1], wb.at[1, pl.ds(0, 960)]),
        "w2": load(9, w_hbm.at[2], wb.at[2, pl.ds(0, 960)]),
    }
    for name in loads:
        loads[name].start()

    barrier = pltpu.get_barrier_semaphore()
    peers = [space_peer(d) for d in range(1, SPACE)] + [dp_peer(d) for d in range(1, DP)]
    peers.append(device_at(x, y, 3 - z, core))
    for peer in peers:
        pl.semaphore_signal(barrier, inc=1, device_id=peer, device_id_type=MESH)

    for i in range(3):
        wb[i, pl.ds(960, 64), :] = jnp.zeros((64, CH), BF16)
        wt[i, pl.ds(960, 64), :] = jnp.zeros((64, CH), BF16)

    @pl.when(sp == 0)
    def _():
        gb[pl.ds(0, COLS), :] = jnp.zeros((COLS, CH), BF16)

    @pl.when(sp == SPACE - 1)
    def _():
        gb[pl.ds(5 * COLS, COLS), :] = jnp.zeros((COLS, CH), BF16)

    loads["x"].wait()
    loads["g"].wait()
    pl.semaphore_wait(barrier, len(peers))

    first, last = pl.ds(COLS, COLS), pl.ds(4 * COLS, COLS)
    above, below = pl.ds(0, COLS), pl.ds(5 * COLS, COLS)
    up = (dp, lax.max(sp - 1, 0))
    down = (dp, lax.min(sp + 1, SPACE - 1))
    g_up = remote(HALO, gb.at[first], gb.at[below], up)
    g_down = remote(HALO + 1, gb.at[last], gb.at[above], down)
    x_up = remote(HALO + 2, xb.at[first], xb.at[below], up)
    x_down = remote(HALO + 3, xb.at[last], xb.at[above], down)

    @pl.when(sp > 0)
    def _():
        g_up.start()
        x_up.start()

    @pl.when(sp < SPACE - 1)
    def _():
        g_down.start()
        x_down.start()

    step = 64

    def sums(k, carry):
        at_rows = pl.ds(pl.multiple_of(COLS + k * step, step), step)
        xs = xb[at_rows, :].astype(F32).reshape(step // 8, 8, CH)
        gs = gb[at_rows, :].astype(F32).reshape(step // 8, 8, CH)
        return carry[0] + jnp.sum(xs, axis=0), carry[1] + jnp.sum(gs, axis=0)

    zero8 = jnp.zeros((8, CH), F32)
    x_sum, g_sum = lax.fori_loop(0, CELLS // step, sums, (zero8, zero8))
    x_mean = jnp.sum(x_sum, axis=0, keepdims=True) * (1.0 / CELLS)
    g_total = jnp.sum(g_sum, axis=0, keepdims=True)

    def squares(k, carry):
        at_rows = pl.ds(pl.multiple_of(COLS + k * step, step), step)
        xs = xb[at_rows, :].astype(F32) - x_mean
        return carry + jnp.sum((xs * xs).reshape(step // 8, 8, CH), axis=0)

    x_m2 = jnp.sum(lax.fori_loop(0, CELLS // step, squares, zero8), axis=0, keepdims=True)
    st_out[0, :, pl.ds(0, CH)] = x_mean
    st_out[0, :, pl.ds(384, CH)] = x_m2
    st_out[0, :, pl.ds(768, CH)] = g_total

    def gather_space(base, out, rx):
        return [
            remote(base + d - 1, out.at[0], rx.at[sp], space_peer(d)) for d in range(1, SPACE)
        ]

    stats = gather_space(STATS, st_out, st_rx)
    for copy in stats:
        copy.start()
    st_rx[sp] = st_out[0]

    at_col = lax.broadcasted_iota(jnp.int32, (COLS, CH), 0)

    def three(row, towards):
        before = jnp.where(at_col == 0, 0.0, pltpu.roll(row, 1, 0))
        after = jnp.where(at_col == COLS - 1, 0.0, pltpu.roll(row, COLS - 1, 0))
        pieces = (before, row, after) if towards else (after, row, before)
        return jnp.concatenate(
            [*pieces, jnp.zeros((COLS, 64), F32)], axis=1
        ).astype(BF16)

    def spread_g(k, carry):
        at_rows = pl.ds(pl.multiple_of(k * COLS, COLS), COLS)
        g3[at_rows, :] = three(gb[at_rows, :].astype(F32), False)
        return carry

    lax.fori_loop(1, 5, spread_g, 0)
    for name in ("w0", "w1", "w2"):
        loads[name].wait()

    def turn(k, carry):
        i, j = lax.div(k, 3), lax.rem(k, 3)
        rows = pl.ds(pl.multiple_of(j * CH, CH), CH)
        wt[i, rows, :] = wb[i, rows, :].astype(F32).T.astype(BF16)
        return carry

    lax.fori_loop(0, 9, turn, 0)

    @pl.when(sp > 0)
    def _():
        g_up.wait_send()
        g_down.wait_recv()

    @pl.when(sp < SPACE - 1)
    def _():
        g_down.wait_send()
        g_up.wait_recv()

    spread_g(0, 0)
    spread_g(5, 0)

    row_of = lax.broadcasted_iota(jnp.int32, (CH, CH), 0)
    col_of = lax.broadcasted_iota(jnp.int32, (CH, CH), 1)
    same = (lax.shift_right_logical(row_of * 6554, 16) == lax.shift_right_logical(col_of * 6554, 16))
    member = same.astype(F32)

    def over_group(rows):
        return jnp.dot(
            jnp.broadcast_to(rows, (8, CH)), member,
            precision=lax.Precision.HIGHEST, preferred_element_type=F32,
        )[0:1]

    for name in ("gain", "nbias", "cbias", "emb", "tw"):
        loads[name].wait()
    for copy in stats:
        copy.wait()
    means = [st_rx[s, :, pl.ds(0, CH)] for s in range(SPACE)]
    total = means[0]
    for s in range(1, SPACE):
        total = total + means[s]
    mean = over_group(total) * (1.0 / (SPACE * PER_GROUP))
    spread = jnp.zeros((1, CH), F32)
    g_all = jnp.zeros((1, CH), F32)
    for s in range(SPACE):
        away = means[s] - mean
        spread = spread + (st_rx[s, :, pl.ds(384, CH)] + float(CELLS) * (away * away))
        g_all = g_all + st_rx[s, :, pl.ds(768, CH)]
    var = over_group(spread) * (1.0 / (SPACE * PER_GROUP * CELLS))
    inv = lax.rsqrt(var + EPSILON)
    mean_s[...] = mean
    inv_s[...] = inv
    gains, nbiases = gain[...], nbias[...]

    tm_out[0, :, pl.ds(0, CH)] = emb[...]
    tm_out[0, :, pl.ds(384, CH)] = g_all
    times = [
        remote(TIME + d - 1, tm_out.at[0], tm_rx.at[dp], dp_peer(d)) for d in range(1, DP)
    ]
    for copy in times:
        copy.start()
    tm_rx[dp] = tm_out[0]

    def activate(k):
        at_rows = pl.ds(pl.multiple_of(k * COLS, COLS), COLS)
        shifted = (xb[at_rows, :].astype(F32) - mean) * inv * gains + nbiases
        return shifted * jax.nn.sigmoid(shifted)

    def spread_a(k, carry):
        act = activate(k)
        a3[pl.ds(pl.multiple_of(k * COLS, COLS), COLS), :] = three(act, True)
        at[:, pl.ds(pl.multiple_of((k - 1) * COLS, COLS), COLS)] = act.T.astype(BF16)
        return carry

    lax.fori_loop(1, 5, spread_a, 0)

    orders = (("x", "y", "z"), ("y", "z", "x"), ("z", "x", "y"))
    mine = pl.ds(core * 4, 4)
    theirs = pl.ds(other * 4, 4)

    def stage(number, c):
        base = REDUCE + c * PER_COLOUR
        first_axis, second_axis, third_axis = orders[c]
        qa, qb, qc = place[first_axis], place[second_axis], place[third_axis]
        if number == 0:
            return [remote(base, wg.at[c, :, theirs], rx0.at[c], partner)]
        if number == 6:
            return [remote(base + 16, res.at[c, :, mine], res.at[c, :, mine], partner)]
        copies = []
        for d in range(1, 4):
            n = base + 1 + (number - 1) * 3 + d - 1
            if number == 1:
                to, device = along(first_axis, d)
                copies.append(remote(n, wg.at[c, to, mine], rx1.at[c, d - 1], device))
            elif number == 2:
                to, device = along(second_axis, d)
                copies.append(remote(n, s1.at[c, to], rx2.at[c, d - 1], device))
            elif number == 3:
                to, device = along(third_axis, d)
                copies.append(remote(n, s2.at[c], rx3.at[c, qc], device))
            elif number == 4:
                to, device = along(second_axis, d)
                copies.append(remote(n, fin.at[c], res.at[c, qa, core * 4 + qb], device))
            else:
                to, device = along(first_axis, d)
                piece = res.at[c, qa, mine]
                copies.append(remote(n, piece, piece, device))
        return copies

    def start(number, c):
        for copy in stage(number, c):
            copy.start()

    def event(number, c):
        first_axis, second_axis, third_axis = orders[c]
        qa, qb, qc = place[first_axis], place[second_axis], place[third_axis]
        for copy in stage(number, c):
            copy.wait()
        if number == 0:
            wg[c, :, mine] = wg[c, :, mine] + rx0[c]
        elif number == 1:
            s1[c] = wg[c, qa, mine] + rx1[c, 0] + rx1[c, 1] + rx1[c, 2]
        elif number == 2:
            total = s1[c, qb] + rx2[c, 0] + rx2[c, 1] + rx2[c, 2]
            s2[c] = total
            rx3[c, qc] = total
        elif number == 3:
            total = rx3[c, 0] + rx3[c, 1] + rx3[c, 2] + rx3[c, 3]
            fin[c] = total
            res[c, qa, core * 4 + qb] = total
        if number < 6:
            start(number + 1, c)
        else:
            q = [res[c, n].reshape(CH, 256) for n in range(4)]
            wgo[c, 0] = jnp.concatenate([q[0], q[1][:, :64]], axis=1)
            wgo[c, 1] = jnp.concatenate([q[1][:, 64:], q[2][:, :128]], axis=1)
            wgo[c, 2] = jnp.concatenate([q[2][:, 128:], q[3][:, :192]], axis=1)
            load(10 + c, wgo.at[c], wg_hbm.at[c]).start()

    def weight_part(c):
        def quarter(n, carry):
            lanes = pl.ds(pl.multiple_of(n * 256, 256), 256)
            part = jnp.dot(
                at[...], g3[pl.ds((2 - c) * COLS, CELLS), lanes], preferred_element_type=F32
            )
            wg[c, n] = part.reshape(8, 40, 256)
            return carry

        lax.fori_loop(0, 4, quarter, 0)
        start(0, c)

    for c in range(3):
        weight_part(c)

    @pl.when(sp > 0)
    def _():
        x_up.wait_send()
        x_down.wait_recv()
        a3[pl.ds(0, COLS), :] = three(activate(0), True)

    @pl.when(sp == 0)
    def _():
        a3[pl.ds(0, COLS), :] = jnp.zeros((COLS, 1024), BF16)

    @pl.when(sp < SPACE - 1)
    def _():
        x_down.wait_send()
        x_up.wait_recv()
        a3[pl.ds(5 * COLS, COLS), :] = three(activate(5), True)

    @pl.when(sp == SPACE - 1)
    def _():
        a3[pl.ds(5 * COLS, COLS), :] = jnp.zeros((COLS, 1024), BF16)

    def back_tile(t):
        at_rows = pl.ds(pl.multiple_of(t * TILE, TILE), TILE)
        grad = jnp.zeros((TILE, CH), F32)
        for i in range(3):
            rows = pl.ds(pl.multiple_of(t * TILE + (2 - i) * COLS, TILE), TILE)
            grad = grad + jnp.dot(g3[rows, :], wt[i], preferred_element_type=F32)
        xs = xb[pl.ds(pl.multiple_of(t * TILE + COLS, TILE), TILE), :].astype(F32)
        normed = (xs - mean) * inv
        shifted = normed * gains + nbiases
        sig = jax.nn.sigmoid(shifted)
        n_grad = grad * sig * (1.0 + shifted * (1.0 - sig)) * gains
        ng[at_rows, :] = n_grad
        bacc[0] += jnp.sum(n_grad.reshape(TILE // 8, 8, CH), axis=0)
        bacc[1] += jnp.sum((n_grad * normed).reshape(TILE // 8, 8, CH), axis=0)

    bacc[...] = jnp.zeros((2, 8, CH), F32)
    time_bias = jnp.dot(
        jnp.broadcast_to(emb[...], (16, CH)).astype(BF16), tw[...], preferred_element_type=F32
    )[0:1]

    def out_tile(t):
        at_rows = pl.ds(pl.multiple_of(t * TILE, TILE), TILE)
        conv = jnp.zeros((TILE, CH), F32)
        for i in range(3):
            rows = pl.ds(pl.multiple_of(t * TILE + i * COLS, TILE), TILE)
            conv = conv + jnp.dot(a3[rows, :], wb[i], preferred_element_type=F32)
        xs = xb[pl.ds(pl.multiple_of(t * TILE + COLS, TILE), TILE), :].astype(F32)
        outb[at_rows, :] = (xs + conv + cbias[...] + time_bias).astype(BF16)

    events = [(number, c) for number in range(7) for c in range(3)]

    def back_loop(t, carry):
        back_tile(t)
        for k in range(TILES):
            @pl.when(t == k)
            def _(k=k):
                event(*events[k])
        return carry

    lax.fori_loop(0, TILES, back_loop, 0)
    bk_out[0, :, pl.ds(0, CH)] = jnp.sum(bacc[0], axis=0, keepdims=True)
    bk_out[0, :, pl.ds(384, CH)] = jnp.sum(bacc[1], axis=0, keepdims=True)
    backs = gather_space(BACK, bk_out, bk_rx)
    for copy in backs:
        copy.start()
    bk_rx[sp] = bk_out[0]

    def out_loop(t, carry):
        out_tile(t)
        for k in range(TILES):
            @pl.when(t == k)
            def _(k=k):
                event(*events[TILES + k])
        return carry

    lax.fori_loop(0, TILES, out_loop, 0)
    out_copy = load(13, outb, out_hbm)
    out_copy.start()

    for copy in backs:
        copy.wait()
    first_sum, second_sum = bk_rx[0, :, pl.ds(0, CH)], bk_rx[0, :, pl.ds(384, CH)]
    for s in range(1, SPACE):
        first_sum = first_sum + bk_rx[s, :, pl.ds(0, CH)]
        second_sum = second_sum + bk_rx[s, :, pl.ds(384, CH)]
    scale = 1.0 / (SPACE * PER_GROUP * CELLS)
    first_mean = over_group(first_sum) * scale
    second_mean = over_group(second_sum) * scale

    def grad_tile(t, carry):
        at_rows = pl.ds(pl.multiple_of(t * step, step), step)
        from_rows = pl.ds(pl.multiple_of(t * step + COLS, step), step)
        normed = (xb[from_rows, :].astype(F32) - mean) * inv
        change = inv * (ng[at_rows, :] - first_mean - normed * second_mean)
        lgb[at_rows, :] = (gb[from_rows, :].astype(F32) + change).astype(BF16)
        return carry

    lax.fori_loop(0, CELLS // step, grad_tile, 0)
    lg_copy = load(14, lgb, lg_hbm)
    lg_copy.start()

    for copy in times:
        copy.wait()
    embs = jnp.concatenate([tm_rx[n, :, pl.ds(0, CH)] for n in range(DP)], axis=0)
    grads = jnp.concatenate([tm_rx[n, :, pl.ds(384, CH)] for n in range(DP)], axis=0)
    tgo[...] = lax.dot_general(
        embs, grads, (((0,), (0,)), ((), ())),
        precision=lax.Precision.HIGHEST, preferred_element_type=F32,
    )
    tg_copy = load(15, tgo, tg_hbm)
    tg_copy.start()

    for number, c in events[2 * TILES:]:
        event(number, c)
    for c in range(3):
        load(10 + c, wgo.at[c], wg_hbm.at[c]).wait()
    out_copy.wait()
    lg_copy.wait()
    tg_copy.wait()


def per_device(
    latent, timesteps, norm_gain, norm_bias, conv_weight, conv_bias, time_weight, cotangent
):
    half_count = CH // 2
    frequency = jnp.exp(-math.log(10000.0) * jnp.arange(half_count, dtype=F32) / half_count)
    angles = timesteps.astype(F32)[:, None] * frequency[None, :]
    embedding = jnp.concatenate([jnp.cos(angles), jnp.sin(angles)], axis=1).astype(BF16)
    anywhere = pl.BlockSpec(memory_space=pl.ANY)
    vmem = pltpu.VMEM
    scratch = [
        vmem((6 * COLS, CH), BF16),
        vmem((6 * COLS, CH), BF16),
        vmem((3, 1024, CH), BF16),
        vmem((3, 1024, CH), BF16),
        vmem((CH, CH), BF16),
        vmem((1, CH), F32),
        vmem((1, CH), F32),
        vmem((1, CH), F32),
        vmem((1, CH), F32),
        vmem((6 * COLS, 1024), BF16),
        vmem((6 * COLS, 1024), BF16),
        vmem((CH, CELLS), BF16),
        vmem((CELLS, CH), F32),
        vmem((1, CH), F32),
        vmem((1, CH), F32),
        vmem((CELLS, CH), BF16),
        vmem((CELLS, CH), BF16),
        vmem((3, 3, CH, CH), F32),
        vmem((CH, CH), F32),
        vmem((1, 1, 1152), F32),
        vmem((SPACE, 1, 1152), F32),
        vmem((1, 1, 768), F32),
        vmem((SPACE, 1, 768), F32),
        vmem((1, 1, 768), F32),
        vmem((DP, 1, 768), F32),
        vmem((3, 4, 8, 40, 256), F32),
        vmem((3, 4, 4, 40, 256), F32),
        vmem((3, 3, 4, 40, 256), F32),
        vmem((3, 4, 40, 256), F32),
        vmem((3, 3, 40, 256), F32),
        vmem((3, 40, 256), F32),
        vmem((3, 4, 40, 256), F32),
        vmem((3, 40, 256), F32),
        vmem((3, 4, 8, 40, 256), F32),
        vmem((2, 8, CH), F32),
        pltpu.SemaphoreType.DMA((16,)),
        pltpu.SemaphoreType.DMA((REMOTE,)),
        pltpu.SemaphoreType.DMA((REMOTE,)),
    ]
    out, lg, wgrad, tgrad = pl.pallas_call(
        kernel,
        out_shape=(
            jax.ShapeDtypeStruct((CELLS, CH), BF16),
            jax.ShapeDtypeStruct((CELLS, CH), BF16),
            jax.ShapeDtypeStruct((3, 3, CH, CH), F32),
            jax.ShapeDtypeStruct((CH, CH), F32),
        ),
        in_specs=[anywhere] * 8,
        out_specs=[anywhere] * 4,
        scratch_shapes=scratch,
        compiler_params=pltpu.CompilerParams(
            collective_id=0, has_side_effects=True, vmem_limit_bytes=60 * 1024 * 1024
        ),
        name="block",
    )(
        embedding.astype(F32),
        latent.reshape(CELLS, CH),
        cotangent.reshape(CELLS, CH),
        conv_weight.reshape(3, 3 * CH, CH),
        time_weight,
        norm_gain.reshape(1, CH),
        norm_bias.reshape(1, CH),
        conv_bias.reshape(1, CH),
    )
    shape = latent.shape
    return out.reshape(shape), lg.reshape(shape), wgrad, tgrad


def solution(mesh):
    wide = P("dp", "space", None, None)
    return jax.shard_map(
        per_device,
        mesh=mesh,
        in_specs=(wide, P("dp"), P(), P(), P(), P(), P(), wide),
        out_specs=(wide, wide, P(), P()),
        check_vma=False,
    )
```

time: 328 us -> 93.2 us (0.28); the launches traced: 323 us -> 93 us
  waiting for transfers between devices: 166 us -> 0 us
  Pallas kernels: 0 us -> 73.4 us
  local copies, waits for them, and re-layouts: 55.1 us -> 17.5 us
  matrix products: 33.1 us -> 0 us
  starting transfers between devices: 32.1 us -> 0 us
  other arithmetic: 21.3 us -> 0.69 us
  between operations: 15.5 us -> 1.43 us
    psum x1 -> x0, waiting for transfers between devices: 161 us -> none  [per_device(): weight_grad, time_grad = lax.psum((weight_part, time_part), ('dp', 'space'))]
    pallas_call x0 -> x1, Pallas kernels: none -> 73.4 us  [per_device(): pl.pallas_call(kernel, out_shape=(jax.ShapeDtypeStruct((CELLS, CH), BF16)...]
    dot_general x28 -> x0, matrix products: 33.1 us -> none  [the longest x9 14.2 us: per_device(): jnp.dot(piece.T, grad_flat, preferred_element_type=jnp.float32)]
    slice x20 -> x0, local copies, waits for them, and re-layouts: 22.9 us -> none  [the longest x9 10.8 us: per_device(): padded_grad[:, 2 - tap_row:2 - tap_row + row_count, 2 - tap_col:2 - tap_c...]
    all_to_all x3 -> x0, starting transfers between devices: 21 us -> none  [sent_to_all(): lax.all_to_all(jnp.broadcast_to(value[None], (count, *value.shape)), axis...]
    reduce_sum x11 -> x0, other arithmetic: 13.5 us -> none  [the longest x1 5.78 us: per_device(): grad_total = jnp.sum(cotangent.astype(jnp.float32), axis=(1, 2))]
    ppermute x4 -> x0, starting transfers between devices: 11.1 us -> none  [the longest x2 6.98 us: padded(): lax.ppermute(tail, axis, [(i, (i + 1) % count) for i in range(ends)])]
    reshape x2 -> x3, local copies, waits for them, and re-layouts: 9.36 us -> 3.74 us  [the longest x1 1.25 us: per_device(): conv_bias.reshape(1, CH)]
  transfers between devices with their start and end apart: 8 -> 0, of which waited for: 2 -> 0; matrix products, arithmetic and copies ran while one was open for 3% -> 0% of each run, Pallas kernels for 0% -> 0%
where the time goes in v1:
time: 93.2 us; the launch traced here: 93 us
  Pallas kernels  73.4 us (79%)
  local copies, waits for them, and re-layouts  17.5 us (19%)
  between operations  1.43 us (2%)
    pallas_call x1, Pallas kernels, per_device(): pl.pallas_call(kernel, out_shape=(jax.ShapeDtypeStruct((CELLS, CH), BF16)...  73.4 us
    unnamed x12, local copies, waits for them, and re-layouts  13.7 us

profile of v1, /device:TPU:1, one launch (start us, length us, event | category | flops | bytes accessed | tf_op | source)
XLA Modules:
  0.0 93.0 jit_solution(4412545912699677157)
XLA Ops:
  0.6 0.0 copy-start.1
  1.4 0.1 sine_convert_fusion
  1.5 0.6 maximum_convert_fusion.emb_hbm
  2.1 1.2 %reshape.75.gain_hbm = f32[1,320]{1,0:T(1,128)} reshape(f32[320]{0:T(512)} %param.10) | data formatting | bytes 2560 | tf_op jit(solution)/shard_map/reshape | solution.py:530
  3.4 1.2 %reshape.76.nbias_hbm = f32[1,320]{1,0:T(1,128)} reshape(f32[320]{0:T(512)} %param.11) | data formatting | bytes 2560 | tf_op jit(solution)/shard_map/reshape | solution.py:531
  4.6 1.3 %reshape.77.cbias_hbm = f32[1,320]{1,0:T(1,128)} reshape(f32[320]{0:T(512)} %param.13) | data formatting | bytes 2560 | tf_op jit(solution)/shard_map/reshape | solution.py:532
  5.8 2.5 %copy.12 = bf16[1,4,512,320]{3,2,1,0:T(8,128)(2,1)} copy(bf16[1,4,512,320]{2,3,1,0:T(8,128)(2,1)} %param.8) | data formatting | bytes 2621440 | tf_op args[0]
  8.4 0.0 copy-done.1
  8.4 1.6 %copy.13 = bf16[1,4,512,320]{3,2,1,0:T(8,128)(2,1)} copy(bf16[1,4,512,320]{2,3,1,0:T(8,128)(2,1)S(1)} %copy-done.1) | data formatting | bytes 2621440 | tf_op args[7]
  10.0 73.4 %block.1 = (bf16[2048,320]{1,0:T(8,128)(2,1)}, bf16[2048,320]{1,0:T(8,128)(2,1)}, f32[3,3,320,320]{3,2,1,0:T(8,128)}, f32[320,320]{1,0:T(8,128)}) custom-call(f32[1,320]{1,0:T(1,128)} %maximum_convert_fusion.emb_hbm, bf16[2048,320]{1,0:T(8,128)(2,1)} %bitcast.6, bf16[2048,320]{1,0:T(8,128)(2,1)} %bitcast.7, bf16[3,960,320]{2,1,0:T(8,128)(2,1)} %bitcast.8, ...), custom_call_target="tpu_custom_call" | custom-call | tf_op jit(solution)/shard_map/block/pallas_call | solution.py:509
  83.4 0.0 copy-start
  83.4 2.6 %copy.14 = bf16[1,4,512,320]{2,3,1,0:T(8,128)(2,1)} copy(bf16[1,4,512,320]{3,2,1,0:T(8,128)(2,1)} %bitcast.10) | data formatting | bytes 2621440
  86.0 0.0 copy-done
  86.0 1.5 %copy.15 = bf16[1,4,512,320]{2,3,1,0:T(8,128)(2,1)} copy(bf16[1,4,512,320]{3,2,1,0:T(8,128)(2,1)S(1)} %bitcast.9) | data formatting | bytes 2621440
  87.6 0.0 copy-start.2
  87.6 4.7 %copy.19 = f32[3,3,320,320]{3,2,1,0:T(8,128)} copy(f32[3,3,320,320]{3,2,1,0:T(8,128)} %get-tuple-element.24) | data formatting | bytes 7372800
  92.2 0.0 copy-done.2
  92.2 0.8 copy.20
  (2 shorter events, 0.0 us)
Async XLA Ops:
  0.6 7.8 %copy-start.1 = (bf16[1,4,512,320]{2,3,1,0:T(8,128)(2,1)S(1)}, bf16[1,4,512,320]{2,3,1,0:T(8,128)(2,1)}, u32[]{:S(2)}) copy-start(bf16[1,4,512,320]{2,3,1,0:T(8,128)(2,1)} %param.15) | copy-start | bytes 3932164
  83.4 2.6 %copy-start = (bf16[2048,320]{1,0:T(8,128)(2,1)S(1)}, bf16[2048,320]{1,0:T(8,128)(2,1)}, u32[]{:S(2)}) copy-start(bf16[2048,320]{1,0:T(8,128)(2,1)} %get-tuple-element.9) | copy-start | bytes 3932164
  87.6 4.7 %copy-start.2 = (f32[320,320]{1,0:T(8,128)S(1)}, f32[320,320]{1,0:T(8,128)}, u32[]{:S(2)}) copy-start(f32[320,320]{1,0:T(8,128)} %get-tuple-element.25) | copy-start | bytes 1228804

commit v2 on v1

v2 whole, which is shorter than its diff:
```python
import math

import jax
import jax.numpy as jnp
from jax import lax
from jax.experimental import pallas as pl
from jax.experimental.pallas import tpu as pltpu
from jax.sharding import PartitionSpec as P

GROUPS = 32
EPSILON = 1e-05
CH = 320
ROWS = 4
COLS = 512
CELLS = ROWS * COLS
PER_GROUP = CH // GROUPS
SPACE = 16
DP = 8
DEEP = 1024
MESH = pl.DeviceIdType.MESH
F32 = jnp.float32
BF16 = jnp.bfloat16

HALO = 0
STATS = 4
BACK = STATS + 15
TIME = BACK + 15
REDUCE = TIME + 7
PER_COLOUR = 17
REMOTE = REDUCE + 3 * PER_COLOUR


def device_at(x, y, z, core):
    return (x * 2 + lax.rem(z, 2), lax.div(z, 2) * 8 + y * 2 + core)


def kernel(
    emb_hbm, x_hbm, g_hbm, w_hbm, tw_hbm, gain_hbm, nbias_hbm, cbias_hbm,
    outb, lgb, wgo, tgo,
    xb, gb, wb, tw, emb, gain, nbias, cbias,
    wgl, wcl, gt, g3, a3, at, act_s, ng, cols,
    st_out, st_rx, bk_out, bk_rx, tm_out, tm_rx,
    wg, rx0, rx1, s1, rx2, s2, rx3, fin, res,
    sums, local, send, recv,
):
    dp = lax.axis_index("dp")
    sp = lax.axis_index("space")
    x = lax.div(dp, 2)
    z = lax.div(sp, 8) * 2 + lax.rem(dp, 2)
    y = lax.rem(lax.div(sp, 2), 4)
    core = lax.rem(sp, 2)
    other = 1 - core
    place = {"x": x, "y": y, "z": z}

    def along(axis, d):
        spot = dict(place)
        spot[axis] = lax.rem(place[axis] + d, 4)
        return spot[axis], device_at(spot["x"], spot["y"], spot["z"], core)

    def space_peer(d):
        return (dp, lax.rem(sp + d, SPACE))

    def dp_peer(d):
        return (lax.rem(dp + d, DP), sp)

    partner = (dp, sp + 1 - 2 * core)

    def remote(number, src, dst, device):
        return pltpu.make_async_remote_copy(
            src_ref=src, dst_ref=dst, send_sem=send.at[number], recv_sem=recv.at[number],
            device_id=device, device_id_type=MESH,
        )

    def load(number, src, dst):
        return pltpu.make_async_copy(src, dst, local.at[number])

    loads = {
        "x": load(0, x_hbm, xb.at[pl.ds(1, ROWS)]),
        "g": load(1, g_hbm, gb.at[pl.ds(1, ROWS)]),
        "tw": load(2, tw_hbm, tw),
        "emb": load(3, emb_hbm, emb),
        "gain": load(4, gain_hbm, gain),
        "nbias": load(5, nbias_hbm, nbias),
        "cbias": load(6, cbias_hbm, cbias),
        "w": load(7, w_hbm, wb),
    }
    for name in loads:
        loads[name].start()

    barrier = pltpu.get_barrier_semaphore()
    peers = [space_peer(d) for d in range(1, SPACE)] + [dp_peer(d) for d in range(1, DP)]
    peers.append(device_at(x, y, 3 - z, core))
    for peer in peers:
        pl.semaphore_signal(barrier, inc=1, device_id=peer, device_id_type=MESH)

    for slot in range(ROWS + 2):
        rows = pl.ds(slot * DEEP + 3 * CH, DEEP - 3 * CH)
        g3[rows, :] = jnp.zeros((DEEP - 3 * CH, COLS), BF16)
        a3[rows, :] = jnp.zeros((DEEP - 3 * CH, COLS), BF16)

    @pl.when(sp == 0)
    def _():
        gb[0] = jnp.zeros((CH, COLS), BF16)

    @pl.when(sp == SPACE - 1)
    def _():
        gb[ROWS + 1] = jnp.zeros((CH, COLS), BF16)

    loads["x"].wait()
    loads["g"].wait()
    pl.semaphore_wait(barrier, len(peers))

    up = (dp, lax.max(sp - 1, 0))
    down = (dp, lax.min(sp + 1, SPACE - 1))
    g_up = remote(HALO, gb.at[1], gb.at[ROWS + 1], up)
    g_down = remote(HALO + 1, gb.at[ROWS], gb.at[0], down)
    x_up = remote(HALO + 2, xb.at[1], xb.at[ROWS + 1], up)
    x_down = remote(HALO + 3, xb.at[ROWS], xb.at[0], down)

    @pl.when(sp > 0)
    def _():
        g_up.start()
        x_up.start()

    @pl.when(sp < SPACE - 1)
    def _():
        g_down.start()
        x_down.start()

    block = 80

    def local_sums(k, carry):
        rows = pl.ds(pl.multiple_of(k * block, block), block)

        def lane_tiles(ref):
            for r in range(1, ROWS + 1):
                row = ref[r, rows, :].astype(F32)
                for n in range(COLS // 128):
                    yield row[:, n * 128 : (n + 1) * 128]

        x_sum = sum(lane_tiles(xb), jnp.zeros((block, 128), F32))
        x_mean = jnp.sum(x_sum, axis=1, keepdims=True) * (1.0 / CELLS)
        sums[0, rows, :] = jnp.broadcast_to(x_mean, (block, 128))
        squares = jnp.zeros((block, 128), F32)
        for piece in lane_tiles(xb):
            away = piece - x_mean
            squares = squares + away * away
        sums[1, rows, :] = squares
        sums[2, rows, :] = sum(lane_tiles(gb), jnp.zeros((block, 128), F32))
        return carry

    lax.fori_loop(0, CH // block, local_sums, 0)
    st_out[0, :, pl.ds(0, CH)] = sums[0].T[0:1]
    st_out[0, :, pl.ds(384, CH)] = jnp.sum(sums[1].T, axis=0, keepdims=True)
    st_out[0, :, pl.ds(768, CH)] = jnp.sum(sums[2].T, axis=0, keepdims=True)

    def gather_space(base, out, rx):
        return [
            remote(base + d - 1, out.at[0], rx.at[sp], space_peer(d)) for d in range(1, SPACE)
        ]

    stats = gather_space(STATS, st_out, st_rx)
    for copy in stats:
        copy.start()
    st_rx[sp] = st_out[0]

    at_col = lax.broadcasted_iota(jnp.int32, (CH, COLS), 1)

    def three(row, towards):
        before = jnp.where(at_col == 0, 0.0, pltpu.roll(row, 1, 1))
        after = jnp.where(at_col == COLS - 1, 0.0, pltpu.roll(row, COLS - 1, 1))
        return (before, row, after) if towards else (after, row, before)

    def spread(ref, k, pieces):
        for j in range(3):
            rows = pl.ds(pl.multiple_of(k * DEEP + j * CH, 64), CH)
            ref[rows, :] = pieces[j].astype(BF16)

    def spread_g(k, carry):
        pieces = three(gb[k].astype(F32), False)
        spread(g3, k, pieces)
        gt[pl.ds(pl.multiple_of(k * COLS, COLS), COLS), :] = jnp.concatenate(
            [*[piece.T for piece in pieces], jnp.zeros((COLS, DEEP - 3 * CH), F32)], axis=1
        ).astype(BF16)
        return carry

    lax.fori_loop(1, ROWS + 1, spread_g, 0)
    loads["w"].wait()

    def lay_out(i, carry):
        taps = wb[i].astype(F32)
        none = jnp.zeros((CH, DEEP - 3 * CH), F32)
        wcl[:, pl.ds(pl.multiple_of(i * DEEP, DEEP), DEEP)] = jnp.concatenate(
            [taps.T, none], axis=1
        ).astype(BF16)
        wgl[:, pl.ds(pl.multiple_of((2 - i) * DEEP, DEEP), DEEP)] = jnp.concatenate(
            [taps[0:CH], taps[CH : 2 * CH], taps[2 * CH :], none], axis=1
        ).astype(BF16)
        return carry

    lax.fori_loop(0, 3, lay_out, 0)

    @pl.when(sp > 0)
    def _():
        g_up.wait_send()
        g_down.wait_recv()

    @pl.when(sp < SPACE - 1)
    def _():
        g_down.wait_send()
        g_up.wait_recv()

    def ends_g(n, carry):
        return spread_g(n * (ROWS + 1), carry)

    lax.fori_loop(0, 2, ends_g, 0)

    row_of = lax.broadcasted_iota(jnp.int32, (CH, CH), 0)
    col_of = lax.broadcasted_iota(jnp.int32, (CH, CH), 1)
    same = (lax.shift_right_logical(row_of * 6554, 16) == lax.shift_right_logical(col_of * 6554, 16))
    member = same.astype(F32)

    def over_group(rows):
        return jnp.dot(
            jnp.broadcast_to(rows, (8, CH)), member,
            precision=lax.Precision.HIGHEST, preferred_element_type=F32,
        )[0:1]

    def to_column(n, rows):
        cols[n] = jnp.broadcast_to(rows, (128, CH)).T

    for name in ("gain", "nbias", "cbias", "emb", "tw"):
        loads[name].wait()
    to_column(0, gain[...].reshape(1, CH))
    to_column(1, nbias[...].reshape(1, CH))
    time_bias = jnp.dot(
        jnp.broadcast_to(emb[...].reshape(1, CH), (16, CH)).astype(BF16), tw[...],
        preferred_element_type=F32,
    )[0:1]
    to_column(2, cbias[...].reshape(1, CH) + time_bias)
    for copy in stats:
        copy.wait()
    means = [st_rx[s, :, pl.ds(0, CH)] for s in range(SPACE)]
    total = means[0]
    for s in range(1, SPACE):
        total = total + means[s]
    mean = over_group(total) * (1.0 / (SPACE * PER_GROUP))
    around = jnp.zeros((1, CH), F32)
    g_all = jnp.zeros((1, CH), F32)
    for s in range(SPACE):
        away = means[s] - mean
        around = around + (st_rx[s, :, pl.ds(384, CH)] + float(CELLS) * (away * away))
        g_all = g_all + st_rx[s, :, pl.ds(768, CH)]
    var = over_group(around) * (1.0 / (SPACE * PER_GROUP * CELLS))
    to_column(3, mean)
    to_column(4, lax.rsqrt(var + EPSILON))

    tm_out[0, :, pl.ds(0, CH)] = emb[...].reshape(1, CH)
    tm_out[0, :, pl.ds(384, CH)] = g_all
    times = [
        remote(TIME + d - 1, tm_out.at[0], tm_rx.at[dp], dp_peer(d)) for d in range(1, DP)
    ]
    for copy in times:
        copy.start()
    tm_rx[dp] = tm_out[0]

    def lanes(n):
        return pl.ds(n * 128, 128)

    def activate(k):
        for n in range(COLS // 128):
            normed = (xb[k, :, lanes(n)].astype(F32) - cols[3]) * cols[4]
            shifted = normed * cols[0] + cols[1]
            act_s[:, lanes(n)] = shifted * jax.nn.sigmoid(shifted)

    def spread_a(k, carry):
        activate(k)
        act = act_s[...]
        spread(a3, k, three(act, True))
        at[:, pl.ds(pl.multiple_of((k - 1) * COLS, COLS), COLS)] = act.astype(BF16)
        return carry

    lax.fori_loop(1, ROWS + 1, spread_a, 0)

    orders = (("x", "y", "z"), ("y", "z", "x"), ("z", "x", "y"))
    mine = pl.ds(core * 4, 4)
    theirs = pl.ds(other * 4, 4)

    def stage(number, c):
        base = REDUCE + c * PER_COLOUR
        first_axis, second_axis, third_axis = orders[c]
        qa, qb, qc = place[first_axis], place[second_axis], place[third_axis]
        if number == 0:
            return [remote(base, wg.at[c, :, theirs], rx0.at[c], partner)]
        if number == 6:
            return [remote(base + 16, res.at[c, :, mine], res.at[c, :, mine], partner)]
        copies = []
        for d in range(1, 4):
            n = base + 1 + (number - 1) * 3 + d - 1
            if number == 1:
                to, device = along(first_axis, d)
                copies.append(remote(n, wg.at[c, to, mine], rx1.at[c, d - 1], device))
            elif number == 2:
                to, device = along(second_axis, d)
                copies.append(remote(n, s1.at[c, to], rx2.at[c, d - 1], device))
            elif number == 3:
                to, device = along(third_axis, d)
                copies.append(remote(n, s2.at[c], rx3.at[c, qc], device))
            elif number == 4:
                to, device = along(second_axis, d)
                copies.append(remote(n, fin.at[c], res.at[c, qa, core * 4 + qb], device))
            else:
                to, device = along(first_axis, d)
                piece = res.at[c, qa, mine]
                copies.append(remote(n, piece, piece, device))
        return copies

    def start(number, c):
        for copy in stage(number, c):
            copy.start()

    def event(number, c):
        first_axis, second_axis, third_axis = orders[c]
        qa, qb, qc = place[first_axis], place[second_axis], place[third_axis]
        for copy in stage(number, c):
            copy.wait()
        if number == 0:
            wg[c, :, mine] = wg[c, :, mine] + rx0[c]
        elif number == 1:
            s1[c] = wg[c, qa, mine] + rx1[c, 0] + rx1[c, 1] + rx1[c, 2]
        elif number == 2:
            total = s1[c, qb] + rx2[c, 0] + rx2[c, 1] + rx2[c, 2]
            s2[c] = total
            rx3[c, qc] = total
        elif number == 3:
            total = rx3[c, 0] + rx3[c, 1] + rx3[c, 2] + rx3[c, 3]
            fin[c] = total
            res[c, qa, core * 4 + qb] = total
        if number < 6:
            start(number + 1, c)
        else:
            q = [res[c, n].reshape(CH, 256) for n in range(4)]
            wgo[c, 0] = jnp.concatenate([q[0], q[1][:, :64]], axis=1)
            wgo[c, 1] = jnp.concatenate([q[1][:, 64:], q[2][:, :128]], axis=1)
            wgo[c, 2] = jnp.concatenate([q[2][:, 128:], q[3][:, :192]], axis=1)

    def weight_part(c):
        def quarter(n, carry):
            part = jnp.dot(
                at[...],
                gt[pl.ds((2 - c) * COLS, CELLS), pl.ds(pl.multiple_of(n * 256, 256), 256)],
                preferred_element_type=F32,
            )
            wg[c, n] = part.reshape(8, 40, 256)
            return carry

        lax.fori_loop(0, 4, quarter, 0)
        start(0, c)

    for c in range(3):
        weight_part(c)

    def edge_a(k):
        activate(k)
        spread(a3, k, three(act_s[...], True))

    def blank_a(k):
        a3[pl.ds(k * DEEP, 3 * CH), :] = jnp.zeros((3 * CH, COLS), BF16)

    @pl.when(sp > 0)
    def _():
        x_up.wait_send()
        x_down.wait_recv()
        edge_a(0)

    @pl.when(sp == 0)
    def _():
        blank_a(0)

    @pl.when(sp < SPACE - 1)
    def _():
        x_down.wait_send()
        x_up.wait_recv()
        edge_a(ROWS + 1)

    @pl.when(sp == SPACE - 1)
    def _():
        blank_a(ROWS + 1)

    wide = 256
    tiles = CELLS // wide

    def spot(t):
        row = lax.div(t, 2)
        return row, pl.multiple_of(lax.rem(t, 2) * wide, wide)

    def convolve(left, right, t):
        row, col = spot(t)
        rows = pl.ds(pl.multiple_of(row * DEEP, DEEP), 3 * DEEP)
        return jnp.dot(left[...], right[rows, pl.ds(col, wide)], preferred_element_type=F32)

    def back_tile(t):
        row, col = spot(t)
        grad = convolve(wgl, g3, t)
        for n in range(wide // 128):
            here = pl.ds(col + n * 128, 128)
            normed = (xb[row + 1, :, here].astype(F32) - cols[3]) * cols[4]
            shifted = normed * cols[0] + cols[1]
            sig = jax.nn.sigmoid(shifted)
            n_grad = (
                grad[:, n * 128 : (n + 1) * 128] * sig * (1.0 + shifted * (1.0 - sig)) * cols[0]
            )
            ng[row, :, here] = n_grad
            sums[0] += n_grad
            sums[1] += n_grad * normed

    sums[0] = jnp.zeros((CH, 128), F32)
    sums[1] = jnp.zeros((CH, 128), F32)

    def out_tile(t):
        row, col = spot(t)
        conv = convolve(wcl, a3, t)
        for n in range(wide // 128):
            here = pl.ds(col + n * 128, 128)
            xs = xb[row + 1, :, here].astype(F32)
            outb[row, :, here] = (xs + conv[:, n * 128 : (n + 1) * 128] + cols[2]).astype(BF16)

    events = [(number, c) for number in range(7) for c in range(3)]

    def back_loop(t, carry):
        back_tile(t)
        for k in range(tiles):
            @pl.when(t == k)
            def _(k=k):
                event(*events[k])
        return carry

    lax.fori_loop(0, tiles, back_loop, 0)
    bk_out[0, :, pl.ds(0, CH)] = jnp.sum(sums[0].T, axis=0, keepdims=True)
    bk_out[0, :, pl.ds(384, CH)] = jnp.sum(sums[1].T, axis=0, keepdims=True)
    backs = gather_space(BACK, bk_out, bk_rx)
    for copy in backs:
        copy.start()
    bk_rx[sp] = bk_out[0]

    def out_loop(t, carry):
        out_tile(t)
        for k in range(tiles):
            @pl.when(t == k)
            def _(k=k):
                event(*events[tiles + k])
        return carry

    lax.fori_loop(0, tiles, out_loop, 0)

    for copy in backs:
        copy.wait()
    first_sum, second_sum = bk_rx[0, :, pl.ds(0, CH)], bk_rx[0, :, pl.ds(384, CH)]
    for s in range(1, SPACE):
        first_sum = first_sum + bk_rx[s, :, pl.ds(0, CH)]
        second_sum = second_sum + bk_rx[s, :, pl.ds(384, CH)]
    scale = 1.0 / (SPACE * PER_GROUP * CELLS)
    to_column(5, over_group(first_sum) * scale)
    to_column(6, over_group(second_sum) * scale)

    def grad_row(row, carry):
        for n in range(COLS // 128):
            normed = (xb[row + 1, :, lanes(n)].astype(F32) - cols[3]) * cols[4]
            change = cols[4] * (ng[row, :, lanes(n)] - cols[5] - normed * cols[6])
            lgb[row, :, lanes(n)] = (gb[row + 1, :, lanes(n)].astype(F32) + change).astype(BF16)
        return carry

    lax.fori_loop(0, ROWS, grad_row, 0)

    for copy in times:
        copy.wait()
    embs = jnp.concatenate([tm_rx[n, :, pl.ds(0, CH)] for n in range(DP)], axis=0)
    grads = jnp.concatenate([tm_rx[n, :, pl.ds(384, CH)] for n in range(DP)], axis=0)
    tgo[...] = lax.dot_general(
        embs, grads, (((0,), (0,)), ((), ())),
        precision=lax.Precision.HIGHEST, preferred_element_type=F32,
    )

    for number, c in events[2 * tiles:]:
        event(number, c)


def store(out_v, lg_v, wg_v, tg_v, out_hbm, lg_hbm, wg_hbm, tg_hbm, sems):
    pairs = ((wg_v, wg_hbm), (out_v, out_hbm), (lg_v, lg_hbm), (tg_v, tg_hbm))
    copies = [pltpu.make_async_copy(a, b, sems.at[n]) for n, (a, b) in enumerate(pairs)]
    for copy in copies:
        copy.start()
    for copy in copies:
        copy.wait()


def per_device(
    latent, timesteps, norm_gain, norm_bias, conv_weight, conv_bias, time_weight, cotangent
):
    half_count = CH // 2
    frequency = jnp.exp(-math.log(10000.0) * jnp.arange(half_count, dtype=F32) / half_count)
    angles = timesteps.astype(F32)[:, None] * frequency[None, :]
    embedding = jnp.concatenate([jnp.cos(angles), jnp.sin(angles)], axis=1).astype(BF16)
    anywhere = pl.BlockSpec(memory_space=pl.ANY)
    vmem = pltpu.VMEM
    scratch = [
        vmem((ROWS + 2, CH, COLS), BF16),
        vmem((ROWS + 2, CH, COLS), BF16),
        vmem((3, 3 * CH, CH), BF16),
        vmem((CH, CH), BF16),
        vmem((CH,), F32),
        vmem((CH,), F32),
        vmem((CH,), F32),
        vmem((CH,), F32),
        vmem((CH, 3 * DEEP), BF16),
        vmem((CH, 3 * DEEP), BF16),
        vmem(((ROWS + 2) * COLS, DEEP), BF16),
        vmem(((ROWS + 2) * DEEP, COLS), BF16),
        vmem(((ROWS + 2) * DEEP, COLS), BF16),
        vmem((CH, CELLS), BF16),
        vmem((CH, COLS), F32),
        vmem((ROWS, CH, COLS), F32),
        vmem((7, CH, 128), F32),
        vmem((1, 1, 1152), F32),
        vmem((SPACE, 1, 1152), F32),
        vmem((1, 1, 768), F32),
        vmem((SPACE, 1, 768), F32),
        vmem((1, 1, 768), F32),
        vmem((DP, 1, 768), F32),
        vmem((3, 4, 8, 40, 256), F32),
        vmem((3, 4, 4, 40, 256), F32),
        vmem((3, 3, 4, 40, 256), F32),
        vmem((3, 4, 40, 256), F32),
        vmem((3, 3, 40, 256), F32),
        vmem((3, 40, 256), F32),
        vmem((3, 4, 40, 256), F32),
        vmem((3, 40, 256), F32),
        vmem((3, 4, 8, 40, 256), F32),
        vmem((3, CH, 128), F32),
        pltpu.SemaphoreType.DMA((16,)),
        pltpu.SemaphoreType.DMA((REMOTE,)),
        pltpu.SemaphoreType.DMA((REMOTE,)),
    ]
    shapes = (
        ((ROWS, CH, COLS), BF16),
        ((ROWS, CH, COLS), BF16),
        ((3, 3, CH, CH), F32),
        ((CH, CH), F32),
    )
    held = pl.pallas_call(
        kernel,
        out_shape=tuple(vmem(*shape) for shape in shapes),
        in_specs=[anywhere] * 8,
        out_specs=[pl.BlockSpec(memory_space=pltpu.VMEM)] * 4,
        scratch_shapes=scratch,
        compiler_params=pltpu.CompilerParams(
            collective_id=0, has_side_effects=True, vmem_limit_bytes=52 * 1024 * 1024
        ),
        name="block",
    )(
        embedding.astype(F32).reshape(CH),
        jnp.swapaxes(latent, 2, 3).reshape(ROWS, CH, COLS),
        jnp.swapaxes(cotangent, 2, 3).reshape(ROWS, CH, COLS),
        conv_weight.reshape(3, 3 * CH, CH),
        time_weight,
        norm_gain,
        norm_bias,
        conv_bias,
    )
    out, lg, wgrad, tgrad = pl.pallas_call(
        store,
        out_shape=tuple(jax.ShapeDtypeStruct(*shape) for shape in shapes),
        in_specs=[anywhere] * 4,
        out_specs=[anywhere] * 4,
        scratch_shapes=[pltpu.SemaphoreType.DMA((4,))],
        compiler_params=pltpu.CompilerParams(vmem_limit_bytes=1024 * 1024),
        name="store",
    )(*held)
    out = jnp.swapaxes(out.reshape(1, ROWS, CH, COLS), 2, 3)
    lg = jnp.swapaxes(lg.reshape(1, ROWS, CH, COLS), 2, 3)
    return out, lg, wgrad, tgrad


def solution(mesh):
    wide = P("dp", "space", None, None)
    return jax.shard_map(
        per_device,
        mesh=mesh,
        in_specs=(wide, P("dp"), P(), P(), P(), P(), P(), wide),
        out_specs=(wide, wide, P(), P()),
        check_vma=False,
    )
```

time: 93.2 us -> 73.8 us (0.79)
  local copies, waits for them, and re-layouts: 17.5 us -> 0 us
  Pallas kernels: 73.4 us -> 71.6 us
    unnamed x12 -> x0, local copies, waits for them, and re-layouts: 13.7 us -> none
    reshape x3 -> x0, local copies, waits for them, and re-layouts: 3.74 us -> none  [the longest x1 1.25 us: per_device(): conv_bias.reshape(1, CH)]
    pallas_call x1 -> x2, Pallas kernels: 73.4 us -> 71.6 us  [the longest x1 68.6 us: per_device(): pl.pallas_call(kernel, out_shape=tuple((vmem(*shape) for shape in shapes)...]
where the time goes in v2:
time: 73.8 us; the launch traced here: 73.6 us
  Pallas kernels  71.6 us (97%)
  between operations  1.29 us (2%)
    pallas_call x1, Pallas kernels, per_device(): pl.pallas_call(kernel, out_shape=tuple((vmem(*shape) for shape in shapes)...  68.6 us
    pallas_call x1, Pallas kernels, per_device(): pl.pallas_call(store, out_shape=tuple((jax.ShapeDtypeStruct(*shape) for s...  3.06 us

profile of v2, /device:TPU:1, one launch (start us, length us, event | category | flops | bytes accessed | tf_op | source)
XLA Modules:
  0.0 73.6 jit_solution(2236082896561513200)
XLA Ops:
  1.3 0.1 sine_convert_fusion
  1.3 0.7 maximum_convert_fusion.emb_hbm
  2.0 68.6 %block.1 = (bf16[4,320,512]{2,1,0:T(8,128)(2,1)S(1)}, bf16[4,320,512]{2,1,0:T(8,128)(2,1)S(1)}, f32[3,3,320,320]{3,2,1,0:T(8,128)S(1)}, f32[320,320]{1,0:T(8,128)S(1)}) custom-call(f32[320]{0:T(512)} %maximum_convert_fusion.emb_hbm, bf16[4,320,512]{2,1,0:T(8,128)(2,1)} %bitcast.15, bf16[4,320,512]{2,1,0:T(8,128)(2,1)} %bitcast.16, ...), custom_call_target="tpu_custom_call" | custom-call | tf_op jit(solution)/shard_map/block/pallas_call | solution.py:550
  70.6 3.1 %store.1 = (bf16[4,320,512]{2,1,0:T(8,128)(2,1)}, bf16[4,320,512]{2,1,0:T(8,128)(2,1)}, f32[3,3,320,320]{3,2,1,0:T(8,128)}, f32[320,320]{1,0:T(8,128)}) custom-call(bf16[4,320,512]{2,1,0:T(8,128)(2,1)S(1)} %get-tuple-element.12.out_v, bf16[4,320,512]{2,1,0:T(8,128)(2,1)S(1)} %get-tuple-element.13.lg_v, f32[3,3,320,320]{3,2,1,0:T(8,128)S(1)} %get-tuple-element.14.wg_v, ...), custom_call_target="tpu_custom_call" | custom-call | tf_op jit(solution)/shard_map/store/pallas_call | solution.py:570

commit v3 on v2

--- a/solution.py
+++ b/solution.py
@@ -24,10 +24,14 @@
 HALO = 0
 STATS = 4
 BACK = STATS + 15
-TIME = BACK + 15
+COLUMN = BACK + 15
+TIME = COLUMN + 15
 REDUCE = TIME + 7
-PER_COLOUR = 17
-REMOTE = REDUCE + 3 * PER_COLOUR
+PER_FLOW = 17
+REMOTE = REDUCE + 6 * PER_FLOW
+
+HALF_US, TILE_US, EVENT_US = 0.7, 0.5, 0.1
+ARRIVES_US = (1.5, 4.5, 7.0, 9.5, 12.0, 15.0, 17.5)
 
 
 def device_at(x, y, z, core):
@@ -39,8 +43,8 @@
     outb, lgb, wgo, tgo,
     xb, gb, wb, tw, emb, gain, nbias, cbias,
     wgl, wcl, gt, g3, a3, at, act_s, ng, cols,
-    st_out, st_rx, bk_out, bk_rx, tm_out, tm_rx,
-    wg, rx0, rx1, s1, rx2, s2, rx3, fin, res,
+    st_out, st_rx, co_out, co_rx, bk_out, bk_rx, tm_out, tm_rx,
+    wg, rx0, tx1, rx1, s1, rx2, s2, rx3, fin, res,
     sums, local, send, recv,
 ):
     dp = lax.axis_index("dp")
@@ -84,15 +88,15 @@
         "cbias": load(6, cbias_hbm, cbias),
         "w": load(7, w_hbm, wb),
     }
-    for name in loads:
-        loads[name].start()
-
     barrier = pltpu.get_barrier_semaphore()
     peers = [space_peer(d) for d in range(1, SPACE)] + [dp_peer(d) for d in range(1, DP)]
     peers.append(device_at(x, y, 3 - z, core))
     for peer in peers:
         pl.semaphore_signal(barrier, inc=1, device_id=peer, device_id_type=MESH)
 
+    for name in loads:
+        loads[name].start()
+
     for slot in range(ROWS + 2):
         rows = pl.ds(slot * DEEP + 3 * CH, DEEP - 3 * CH)
         g3[rows, :] = jnp.zeros((DEEP - 3 * CH, COLS), BF16)
@@ -107,8 +111,47 @@
         gb[ROWS + 1] = jnp.zeros((CH, COLS), BF16)
 
     loads["x"].wait()
+
+    block = 80
+
+    def lane_tiles(ref, rows):
+        for r in range(1, ROWS + 1):
+            row = ref[r, rows, :].astype(F32)
+            for n in range(COLS // 128):
+                yield row[:, n * 128 : (n + 1) * 128]
+
+    def local_sums(k, carry):
+        rows = pl.ds(pl.multiple_of(k * block, block), block)
+        x_sum = sum(lane_tiles(xb, rows), jnp.zeros((block, 128), F32))
+        x_mean = jnp.sum(x_sum, axis=1, keepdims=True) * (1.0 / CELLS)
+        sums[0, rows, :] = jnp.broadcast_to(x_mean, (block, 128))
+        squares = jnp.zeros((block, 128), F32)
+        for piece in lane_tiles(xb, rows):
+            away = piece - x_mean
+            squares = squares + away * away
+        sums[1, rows, :] = squares
+        return carry
+
+    def local_totals(k, carry):
+        rows = pl.ds(pl.multiple_of(k * block, block), block)
+        sums[2, rows, :] = sum(lane_tiles(gb, rows), jnp.zeros((block, 128), F32))
+        return carry
+
+    lax.fori_loop(0, CH // block, local_sums, 0)
+    st_out[0, :, pl.ds(0, CH)] = sums[0].T[0:1]
+    st_out[0, :, pl.ds(384, CH)] = jnp.sum(sums[1].T, axis=0, keepdims=True)
+
+    def gather_space(base, out, rx):
+        return [
+            remote(base + d - 1, out.at[0], rx.at[sp], space_peer(d)) for d in range(1, SPACE)
+        ]
+
+    stats = gather_space(STATS, st_out, st_rx)
+    pl.semaphore_wait(barrier, len(peers))
+    for copy in stats:
+        copy.start()
+    st_rx[sp] = st_out[0]
     loads["g"].wait()
-    pl.semaphore_wait(barrier, len(peers))
 
     up = (dp, lax.max(sp - 1, 0))
     down = (dp, lax.min(sp + 1, SPACE - 1))
@@ -120,49 +163,26 @@
     @pl.when(sp > 0)
     def _():
         g_up.start()
+
+    @pl.when(sp < SPACE - 1)
+    def _():
+        g_down.start()
+
+    @pl.when(sp > 0)
+    def _():
         x_up.start()
 
     @pl.when(sp < SPACE - 1)
     def _():
-        g_down.start()
         x_down.start()
 
-    block = 80
-
-    def local_sums(k, carry):
-        rows = pl.ds(pl.multiple_of(k * block, block), block)
-
-        def lane_tiles(ref):
-            for r in range(1, ROWS + 1):
-                row = ref[r, rows, :].astype(F32)
-                for n in range(COLS // 128):
-                    yield row[:, n * 128 : (n + 1) * 128]
-
-        x_sum = sum(lane_tiles(xb), jnp.zeros((block, 128), F32))
-        x_mean = jnp.sum(x_sum, axis=1, keepdims=True) * (1.0 / CELLS)
-        sums[0, rows, :] = jnp.broadcast_to(x_mean, (block, 128))
-        squares = jnp.zeros((block, 128), F32)
-        for piece in lane_tiles(xb):
-            away = piece - x_mean
-            squares = squares + away * away
-        sums[1, rows, :] = squares
-        sums[2, rows, :] = sum(lane_tiles(gb), jnp.zeros((block, 128), F32))
-        return carry
-
-    lax.fori_loop(0, CH // block, local_sums, 0)
-    st_out[0, :, pl.ds(0, CH)] = sums[0].T[0:1]
-    st_out[0, :, pl.ds(384, CH)] = jnp.sum(sums[1].T, axis=0, keepdims=True)
-    st_out[0, :, pl.ds(768, CH)] = jnp.sum(sums[2].T, axis=0, keepdims=True)
-
-    def gather_space(base, out, rx):
-        return [
-            remote(base + d - 1, out.at[0], rx.at[sp], space_peer(d)) for d in range(1, SPACE)
-        ]
-
-    stats = gather_space(STATS, st_out, st_rx)
-    for copy in stats:
+    lax.fori_loop(0, CH // block, local_totals, 0)
+    co_out[0, :, :] = jnp.sum(sums[2].T, axis=0, keepdims=True)
+    columns = gather_space(COLUMN, co_out, co_rx)
+    for copy in columns:
         copy.start()
-    st_rx[sp] = st_out[0]
+    co_rx[sp] = co_out[0]
+
 
     at_col = lax.broadcasted_iota(jnp.int32, (CH, COLS), 1)
 
@@ -179,9 +199,9 @@
     def spread_g(k, carry):
         pieces = three(gb[k].astype(F32), False)
         spread(g3, k, pieces)
-        gt[pl.ds(pl.multiple_of(k * COLS, COLS), COLS), :] = jnp.concatenate(
-            [*[piece.T for piece in pieces], jnp.zeros((COLS, DEEP - 3 * CH), F32)], axis=1
-        ).astype(BF16)
+        gt[pl.ds(pl.multiple_of(k * COLS, COLS), COLS), :] = (
+            g3[pl.ds(pl.multiple_of(k * DEEP, DEEP), DEEP), :].T
+        )
         return carry
 
     lax.fori_loop(1, ROWS + 1, spread_g, 0)
@@ -246,15 +266,36 @@
         total = total + means[s]
     mean = over_group(total) * (1.0 / (SPACE * PER_GROUP))
     around = jnp.zeros((1, CH), F32)
-    g_all = jnp.zeros((1, CH), F32)
     for s in range(SPACE):
         away = means[s] - mean
         around = around + (st_rx[s, :, pl.ds(384, CH)] + float(CELLS) * (away * away))
-        g_all = g_all + st_rx[s, :, pl.ds(768, CH)]
     var = over_group(around) * (1.0 / (SPACE * PER_GROUP * CELLS))
     to_column(3, mean)
     to_column(4, lax.rsqrt(var + EPSILON))
 
+    def lanes(n):
+        return pl.ds(n * 128, 128)
+
+    def activate(k):
+        for n in range(COLS // 128):
+            normed = (xb[k, :, lanes(n)].astype(F32) - cols[3]) * cols[4]
+            shifted = normed * cols[0] + cols[1]
+            act_s[:, lanes(n)] = shifted * jax.nn.sigmoid(shifted)
+
+    def spread_a(k, carry):
+        activate(k)
+        act = act_s[...]
+        spread(a3, k, three(act, True))
+        at[:, pl.ds(pl.multiple_of((k - 1) * COLS, COLS), COLS)] = act.astype(BF16)
+        return carry
+
+    lax.fori_loop(1, ROWS + 1, spread_a, 0)
+
+    for copy in columns:
+        copy.wait()
+    g_all = co_rx[0]
+    for n in range(1, SPACE):
+        g_all = g_all + co_rx[n]
     tm_out[0, :, pl.ds(0, CH)] = emb[...].reshape(1, CH)
     tm_out[0, :, pl.ds(384, CH)] = g_all
     times = [
@@ -264,101 +305,118 @@
         copy.start()
     tm_rx[dp] = tm_out[0]
 
-    def lanes(n):
-        return pl.ds(n * 128, 128)
-
-    def activate(k):
-        for n in range(COLS // 128):
-            normed = (xb[k, :, lanes(n)].astype(F32) - cols[3]) * cols[4]
-            shifted = normed * cols[0] + cols[1]
-            act_s[:, lanes(n)] = shifted * jax.nn.sigmoid(shifted)
-
-    def spread_a(k, carry):
-        activate(k)
-        act = act_s[...]
-        spread(a3, k, three(act, True))
-        at[:, pl.ds(pl.multiple_of((k - 1) * COLS, COLS), COLS)] = act.astype(BF16)
-        return carry
-
-    lax.fori_loop(1, ROWS + 1, spread_a, 0)
+    def to_blocks(values):
+        top = jnp.max(jnp.abs(values), axis=1, keepdims=True)
+        power = jnp.ceil(jnp.log2(jnp.maximum(top, 1e-30)) + 0.01)
+        whole = jnp.floor(values * jnp.exp2(15.0 - power) + 0.5)
+        powers = jnp.broadcast_to(power, (values.shape[0], 8, 128))
+        return jnp.concatenate([whole, powers], axis=1).astype(jnp.int32).astype(jnp.int16)
+
+    def from_blocks(blocks):
+        wide_blocks = blocks.astype(jnp.int32).astype(F32)
+        return wide_blocks[:, :40] * jnp.exp2(wide_blocks[:, 40:41] - 15.0)
 
     orders = (("x", "y", "z"), ("y", "z", "x"), ("z", "x", "y"))
     mine = pl.ds(core * 4, 4)
     theirs = pl.ds(other * 4, 4)
 
-    def stage(number, c):
-        base = REDUCE + c * PER_COLOUR
-        first_axis, second_axis, third_axis = orders[c]
-        qa, qb, qc = place[first_axis], place[second_axis], place[third_axis]
+    def axes(f):
+        names = orders[f % 3]
+        return (*names, *[place[name] for name in names])
+
+    def stage(number, f):
+        base = REDUCE + f * PER_FLOW
+        first_axis, second_axis, third_axis, qa, qb, qc = axes(f)
         if number == 0:
-            return [remote(base, wg.at[c, :, theirs], rx0.at[c], partner)]
+            return [remote(base, wg.at[f, :, theirs], rx0.at[f], partner)]
         if number == 6:
-            return [remote(base + 16, res.at[c, :, mine], res.at[c, :, mine], partner)]
+            return [remote(base + 16, res.at[f, :, mine], res.at[f, :, mine], partner)]
         copies = []
         for d in range(1, 4):
             n = base + 1 + (number - 1) * 3 + d - 1
             if number == 1:
                 to, device = along(first_axis, d)
-                copies.append(remote(n, wg.at[c, to, mine], rx1.at[c, d - 1], device))
+                copies.append(remote(n, tx1.at[f, d - 1], rx1.at[f, d - 1], device))
             elif number == 2:
                 to, device = along(second_axis, d)
-                copies.append(remote(n, s1.at[c, to], rx2.at[c, d - 1], device))
+                copies.append(remote(n, s1.at[f, to], rx2.at[f, d - 1], device))
             elif number == 3:
                 to, device = along(third_axis, d)
-                copies.append(remote(n, s2.at[c], rx3.at[c, qc], device))
+                copies.append(remote(n, s2.at[f], rx3.at[f, qc], device))
             elif number == 4:
                 to, device = along(second_axis, d)
-                copies.append(remote(n, fin.at[c], res.at[c, qa, core * 4 + qb], device))
+                copies.append(remote(n, fin.at[f], res.at[f, qa, core * 4 + qb], device))
             else:
                 to, device = along(first_axis, d)
-                piece = res.at[c, qa, mine]
+                piece = res.at[f, qa, mine]
                 copies.append(remote(n, piece, piece, device))
         return copies
 
-    def start(number, c):
-        for copy in stage(number, c):
+    def start(number, f):
+        for copy in stage(number, f):
             copy.start()
 
-    def event(number, c):
-        first_axis, second_axis, third_axis = orders[c]
-        qa, qb, qc = place[first_axis], place[second_axis], place[third_axis]
-        for copy in stage(number, c):
-            copy.wait()
+    def event(number, f):
+        first_axis, second_axis, third_axis, qa, qb, qc = axes(f)
+        for copy in stage(number, f):
+            copy.wait_recv()
         if number == 0:
-            wg[c, :, mine] = wg[c, :, mine] + rx0[c]
+            s1[f] = wg[f, qa, mine] + rx0[f, qa]
+            for d in range(1, 4):
+                to, _ = along(first_axis, d)
+                tx1[f, d - 1] = to_blocks(wg[f, to, mine] + rx0[f, to])
         elif number == 1:
-            s1[c] = wg[c, qa, mine] + rx1[c, 0] + rx1[c, 1] + rx1[c, 2]
+            for d in range(3):
+                s1[f] += from_blocks(rx1[f, d])
         elif number == 2:
-            total = s1[c, qb] + rx2[c, 0] + rx2[c, 1] + rx2[c, 2]
-            s2[c] = total
-            rx3[c, qc] = total
+            total = s1[f, qb] + rx2[f, 0] + rx2[f, 1] + rx2[f, 2]
+            s2[f] = total
+            rx3[f, qc] = total
         elif number == 3:
-            total = rx3[c, 0] + rx3[c, 1] + rx3[c, 2] + rx3[c, 3]
-            fin[c] = total
-            res[c, qa, core * 4 + qb] = total
+            total = rx3[f, 0] + rx3[f, 1] + rx3[f, 2] + rx3[f, 3]
+            block = to_blocks(total[None])[0]
+            fin[f] = block
+            res[f, qa, core * 4 + qb] = block
         if number < 6:
-            start(number + 1, c)
-        else:
-            q = [res[c, n].reshape(CH, 256) for n in range(4)]
-            wgo[c, 0] = jnp.concatenate([q[0], q[1][:, :64]], axis=1)
-            wgo[c, 1] = jnp.concatenate([q[1][:, 64:], q[2][:, :128]], axis=1)
-            wgo[c, 2] = jnp.concatenate([q[2][:, 128:], q[3][:, :192]], axis=1)
-
-    def weight_part(c):
-        def quarter(n, carry):
+            start(number + 1, f)
+        elif f % 2 == 1:
+            c = f // 2
+            part = [from_blocks(res[f - 1 + n // 4, n % 4]).reshape(CH, 128) for n in range(8)]
+            wgo[c, 0] = jnp.concatenate([part[0], part[1], part[2][:, :64]], axis=1)
+            wgo[c, 1] = jnp.concatenate([part[2][:, 64:], part[3], part[4]], axis=1)
+            wgo[c, 2] = jnp.concatenate([part[5], part[6], part[7][:, :64]], axis=1)
+
+    flows = 6
+    due = sorted(
+        (HALF_US * (f + 1) + ARRIVES_US[number], number, f)
+        for number in range(7)
+        for f in range(flows)
+    )
+    clock = [0.0]
+
+    def work(us, do):
+        while due and due[0][0] <= clock[0]:
+            event(*due.pop(0)[1:])
+            clock[0] += EVENT_US
+        do()
+        clock[0] += us
+
+    def weight_part(f):
+        c = f // 2
+        for n in range((f % 2) * 2, (f % 2) * 2 + 2):
             part = jnp.dot(
                 at[...],
-                gt[pl.ds((2 - c) * COLS, CELLS), pl.ds(pl.multiple_of(n * 256, 256), 256)],
+                gt[pl.ds((2 - c) * COLS, CELLS), pl.ds(n * 256, 256)],
                 preferred_element_type=F32,
             )
-            wg[c, n] = part.reshape(8, 40, 256)
-            return carry
-
-        lax.fori_loop(0, 4, quarter, 0)
-        start(0, c)
-
-    for c in range(3):
-        weight_part(c)
+            for side in range(2):
+                wg[f, (n % 2) * 2 + side] = part[:, side * 128 : (side + 1) * 128].reshape(
+                    8, 40, 128
+                )
+        start(0, f)
+
+    for f in range(flows):
+        work(HALF_US, lambda f=f: weight_part(f))
 
     def edge_a(k):
         activate(k)
@@ -367,36 +425,37 @@
     def blank_a(k):
         a3[pl.ds(k * DEEP, 3 * CH), :] = jnp.zeros((3 * CH, COLS), BF16)
 
-    @pl.when(sp > 0)
-    def _():
-        x_up.wait_send()
-        x_down.wait_recv()
-        edge_a(0)
-
-    @pl.when(sp == 0)
-    def _():
-        blank_a(0)
-
-    @pl.when(sp < SPACE - 1)
-    def _():
-        x_down.wait_send()
-        x_up.wait_recv()
-        edge_a(ROWS + 1)
-
-    @pl.when(sp == SPACE - 1)
-    def _():
-        blank_a(ROWS + 1)
+    def top_a():
+        @pl.when(sp > 0)
+        def _():
+            x_up.wait_send()
+            x_down.wait_recv()
+            edge_a(0)
+
+        @pl.when(sp == 0)
+        def _():
+            blank_a(0)
+
+    def bottom_a():
+        @pl.when(sp < SPACE - 1)
+        def _():
+            x_down.wait_send()
+            x_up.wait_recv()
+            edge_a(ROWS + 1)
+
+        @pl.when(sp == SPACE - 1)
+        def _():
+            blank_a(ROWS + 1)
 
     wide = 256
     tiles = CELLS // wide
 
     def spot(t):
-        row = lax.div(t, 2)
-        return row, pl.multiple_of(lax.rem(t, 2) * wide, wide)
+        return t // 2, (t % 2) * wide
 
     def convolve(left, right, t):
         row, col = spot(t)
-        rows = pl.ds(pl.multiple_of(row * DEEP, DEEP), 3 * DEEP)
+        rows = pl.ds(row * DEEP, 3 * DEEP)
         return jnp.dot(left[...], right[rows, pl.ds(col, wide)], preferred_element_type=F32)
 
     def back_tile(t):
@@ -425,64 +484,56 @@
             xs = xb[row + 1, :, here].astype(F32)
             outb[row, :, here] = (xs + conv[:, n * 128 : (n + 1) * 128] + cols[2]).astype(BF16)
 
-    events = [(number, c) for number in range(7) for c in range(3)]
-
-    def back_loop(t, carry):
-        back_tile(t)
-        for k in range(tiles):
-            @pl.when(t == k)
-            def _(k=k):
-                event(*events[k])
-        return carry
-
-    lax.fori_loop(0, tiles, back_loop, 0)
-    bk_out[0, :, pl.ds(0, CH)] = jnp.sum(sums[0].T, axis=0, keepdims=True)
-    bk_out[0, :, pl.ds(384, CH)] = jnp.sum(sums[1].T, axis=0, keepdims=True)
-    backs = gather_space(BACK, bk_out, bk_rx)
-    for copy in backs:
-        copy.start()
-    bk_rx[sp] = bk_out[0]
-
-    def out_loop(t, carry):
-        out_tile(t)
-        for k in range(tiles):
-            @pl.when(t == k)
-            def _(k=k):
-                event(*events[tiles + k])
-        return carry
-
-    lax.fori_loop(0, tiles, out_loop, 0)
-
-    for copy in backs:
-        copy.wait()
-    first_sum, second_sum = bk_rx[0, :, pl.ds(0, CH)], bk_rx[0, :, pl.ds(384, CH)]
-    for s in range(1, SPACE):
-        first_sum = first_sum + bk_rx[s, :, pl.ds(0, CH)]
-        second_sum = second_sum + bk_rx[s, :, pl.ds(384, CH)]
-    scale = 1.0 / (SPACE * PER_GROUP * CELLS)
-    to_column(5, over_group(first_sum) * scale)
-    to_column(6, over_group(second_sum) * scale)
-
-    def grad_row(row, carry):
+    def send_back():
+        bk_out[0, :, pl.ds(0, CH)] = jnp.sum(sums[0].T, axis=0, keepdims=True)
+        bk_out[0, :, pl.ds(384, CH)] = jnp.sum(sums[1].T, axis=0, keepdims=True)
+        for copy in gather_space(BACK, bk_out, bk_rx):
+            copy.start()
+        bk_rx[sp] = bk_out[0]
+
+    def take_back():
+        for copy in gather_space(BACK, bk_out, bk_rx):
+            copy.wait()
+        scale = 1.0 / (SPACE * PER_GROUP * CELLS)
+        for n in range(2):
+            total = bk_rx[0, :, pl.ds(n * 384, CH)]
+            for s in range(1, SPACE):
+                total = total + bk_rx[s, :, pl.ds(n * 384, CH)]
+            to_column(5 + n, over_group(total) * scale)
+
+    def grad_row(row):
         for n in range(COLS // 128):
             normed = (xb[row + 1, :, lanes(n)].astype(F32) - cols[3]) * cols[4]
             change = cols[4] * (ng[row, :, lanes(n)] - cols[5] - normed * cols[6])
             lgb[row, :, lanes(n)] = (gb[row + 1, :, lanes(n)].astype(F32) + change).astype(BF16)
-        return carry
-
-    lax.fori_loop(0, ROWS, grad_row, 0)
-
-    for copy in times:
-        copy.wait()
-    embs = jnp.concatenate([tm_rx[n, :, pl.ds(0, CH)] for n in range(DP)], axis=0)
-    grads = jnp.concatenate([tm_rx[n, :, pl.ds(384, CH)] for n in range(DP)], axis=0)
-    tgo[...] = lax.dot_general(
-        embs, grads, (((0,), (0,)), ((), ())),
-        precision=lax.Precision.HIGHEST, preferred_element_type=F32,
-    )
-
-    for number, c in events[2 * tiles:]:
-        event(number, c)
+
+    def time_gradient():
+        for copy in times:
+            copy.wait()
+        embs = jnp.concatenate([tm_rx[n, :, pl.ds(0, CH)] for n in range(DP)], axis=0)
+        grads = jnp.concatenate([tm_rx[n, :, pl.ds(384, CH)] for n in range(DP)], axis=0)
+        tgo[...] = lax.dot_general(
+            embs, grads, (((0,), (0,)), ((), ())),
+            precision=lax.Precision.HIGHEST, preferred_element_type=F32,
+        )
+
+    for t in range(tiles):
+        work(TILE_US, lambda t=t: back_tile(t))
+    work(1.0, send_back)
+    work(0.5, top_a)
+    work(0.5, bottom_a)
+    for t in range(tiles):
+        work(TILE_US, lambda t=t: out_tile(t))
+    work(1.0, take_back)
+    for row in range(ROWS):
+        work(0.4, lambda row=row: grad_row(row))
+    work(1.0, time_gradient)
+    while due:
+        event(*due.pop(0)[1:])
+    for f in range(flows):
+        for number in range(7):
+            for copy in stage(number, f):
+                copy.wait_send()
 
 
 def store(out_v, lg_v, wg_v, tg_v, out_hbm, lg_hbm, wg_hbm, tg_hbm, sems):
@@ -521,21 +572,24 @@
         vmem((CH, COLS), F32),
         vmem((ROWS, CH, COLS), F32),
         vmem((7, CH, 128), F32),
-        vmem((1, 1, 1152), F32),
-        vmem((SPACE, 1, 1152), F32),
+        vmem((1, 1, 768), F32),
+        vmem((SPACE, 1, 768), F32),
+        vmem((1, 1, CH), F32),
+        vmem((SPACE, 1, CH), F32),
         vmem((1, 1, 768), F32),
         vmem((SPACE, 1, 768), F32),
         vmem((1, 1, 768), F32),
         vmem((DP, 1, 768), F32),
-        vmem((3, 4, 8, 40, 256), F32),
-        vmem((3, 4, 4, 40, 256), F32),
-        vmem((3, 3, 4, 40, 256), F32),
-        vmem((3, 4, 40, 256), F32),
-        vmem((3, 3, 40, 256), F32),
-        vmem((3, 40, 256), F32),
-        vmem((3, 4, 40, 256), F32),
-        vmem((3, 40, 256), F32),
-        vmem((3, 4, 8, 40, 256), F32),
+        vmem((6, 4, 8, 40, 128), F32),
+        vmem((6, 4, 4, 40, 128), F32),
+        vmem((6, 3, 4, 48, 128), jnp.int16),
+        vmem((6, 3, 4, 48, 128), jnp.int16),
+        vmem((6, 4, 40, 128), F32),
+        vmem((6, 3, 40, 128), F32),
+        vmem((6, 40, 128), F32),
+        vmem((6, 4, 40, 128), F32),
+        vmem((6, 48, 128), jnp.int16),
+        vmem((6, 4, 8, 48, 128), jnp.int16),
         vmem((3, CH, 128), F32),
         pltpu.SemaphoreType.DMA((16,)),
         pltpu.SemaphoreType.DMA((REMOTE,)),

time: 73.8 us -> 63.5 us (0.86)
  Pallas kernels: 71.6 us -> 61.2 us
    pallas_call x1, Pallas kernels: 68.6 us -> 58.2 us  [per_device(): pl.pallas_call(kernel, out_shape=tuple((vmem(*shape) for shape in shapes)...]
where the time goes in v3:
time: 63.5 us; the launch traced here: 63.4 us
  Pallas kernels  61.2 us (96%)
  between operations  1.47 us (2%)
  other arithmetic  0.71 us (1%)
    pallas_call x1, Pallas kernels, per_device(): pl.pallas_call(kernel, out_shape=tuple((vmem(*shape) for shape in shapes)...  58.2 us
    pallas_call x1, Pallas kernels, per_device(): pl.pallas_call(store, out_shape=tuple((jax.ShapeDtypeStruct(*shape) for s...  3.06 us

profile of v3, /device:TPU:1, one launch (start us, length us, event | category | flops | bytes accessed | tf_op | source)
XLA Modules:
  0.0 63.4 jit_solution(12799261406148732845)
XLA Ops:
  1.3 0.1 sine_convert_fusion
  1.3 0.7 %maximum_convert_fusion.emb_hbm = f32[320]{0:T(512)} fusion(bf16[160]{0:T(256)(128)(2,1)S(1)} %get-tuple-element.20, bf16[160]{0:T(256)(128)(2,1)S(1)} %get-tuple-element.21), kind=kLoop, calls=%fused_computation | loop fusion | flops 1280 | bytes 1920 | tf_op jit(solution)/shard_map/convert_element_type | solution.py:615
  2.0 58.2 %block.1 = (bf16[4,320,512]{2,1,0:T(8,128)(2,1)S(1)}, bf16[4,320,512]{2,1,0:T(8,128)(2,1)S(1)}, f32[3,3,320,320]{3,2,1,0:T(8,128)S(1)}, f32[320,320]{1,0:T(8,128)S(1)}) custom-call(f32[320]{0:T(512)} %maximum_convert_fusion.emb_hbm, bf16[4,320,512]{2,1,0:T(8,128)(2,1)} %bitcast.15, bf16[4,320,512]{2,1,0:T(8,128)(2,1)} %bitcast.16, ...), custom_call_target="tpu_custom_call" | custom-call | tf_op jit(solution)/shard_map/block/pallas_call | solution.py:604
  60.2 3.1 %store.1 = (bf16[4,320,512]{2,1,0:T(8,128)(2,1)}, bf16[4,320,512]{2,1,0:T(8,128)(2,1)}, f32[3,3,320,320]{3,2,1,0:T(8,128)}, f32[320,320]{1,0:T(8,128)}) custom-call(bf16[4,320,512]{2,1,0:T(8,128)(2,1)S(1)} %get-tuple-element.12.out_v, bf16[4,320,512]{2,1,0:T(8,128)(2,1)S(1)} %get-tuple-element.13.lg_v, f32[3,3,320,320]{3,2,1,0:T(8,128)S(1)} %get-tuple-element.14.wg_v, ...), custom_call_target="tpu_custom_call" | custom-call | tf_op jit(solution)/shard_map/store/pallas_call | solution.py:624

commit v4 on v3

--- a/solution.py
+++ b/solution.py
@@ -30,8 +30,14 @@
 PER_FLOW = 17
 REMOTE = REDUCE + 6 * PER_FLOW
 
-HALF_US, TILE_US, EVENT_US = 0.7, 0.5, 0.1
-ARRIVES_US = (1.5, 4.5, 7.0, 9.5, 12.0, 15.0, 17.5)
+HALF_US, TILE_US, EVENT_US = 0.45, 0.75, 0.1
+TAP_ROWS = (0, 1, 2)
+ARRIVES_US = (2.0, 7.0, 10.0, 13.0, 16.0, 21.0, 23.5)
+
+
+def from_blocks(blocks):
+    wide_blocks = blocks.astype(jnp.int32).astype(F32)
+    return wide_blocks[:, :40] * jnp.exp2(wide_blocks[:, 40:41] - 15.0)
 
 
 def device_at(x, y, z, core):
@@ -40,11 +46,11 @@
 
 def kernel(
     emb_hbm, x_hbm, g_hbm, w_hbm, tw_hbm, gain_hbm, nbias_hbm, cbias_hbm,
-    outb, lgb, wgo, tgo,
+    outb, lgb, res, tgo,
     xb, gb, wb, tw, emb, gain, nbias, cbias,
     wgl, wcl, gt, g3, a3, at, act_s, ng, cols,
     st_out, st_rx, co_out, co_rx, bk_out, bk_rx, tm_out, tm_rx,
-    wg, rx0, tx1, rx1, s1, rx2, s2, rx3, fin, res,
+    wg, rx0, tx1, rx1, s1, rx2, s2, rx3, fin,
     sums, local, send, recv,
 ):
     dp = lax.axis_index("dp")
@@ -220,20 +226,20 @@
 
     lax.fori_loop(0, 3, lay_out, 0)
 
-    @pl.when(sp > 0)
-    def _():
-        g_up.wait_send()
-        g_down.wait_recv()
-
-    @pl.when(sp < SPACE - 1)
-    def _():
-        g_down.wait_send()
-        g_up.wait_recv()
-
-    def ends_g(n, carry):
-        return spread_g(n * (ROWS + 1), carry)
-
-    lax.fori_loop(0, 2, ends_g, 0)
+    def ends_g():
+        @pl.when(sp > 0)
+        def _():
+            g_up.wait_send()
+            g_down.wait_recv()
+
+        @pl.when(sp < SPACE - 1)
+        def _():
+            g_down.wait_send()
+            g_up.wait_recv()
+
+        lax.fori_loop(0, 2, lambda n, carry: spread_g(n * (ROWS + 1), carry), 0)
+
+    ends_g()
 
     row_of = lax.broadcasted_iota(jnp.int32, (CH, CH), 0)
     col_of = lax.broadcasted_iota(jnp.int32, (CH, CH), 1)
@@ -285,7 +291,6 @@
     def spread_a(k, carry):
         activate(k)
         act = act_s[...]
-        spread(a3, k, three(act, True))
         at[:, pl.ds(pl.multiple_of((k - 1) * COLS, COLS), COLS)] = act.astype(BF16)
         return carry
 
@@ -311,10 +316,6 @@
         whole = jnp.floor(values * jnp.exp2(15.0 - power) + 0.5)
         powers = jnp.broadcast_to(power, (values.shape[0], 8, 128))
         return jnp.concatenate([whole, powers], axis=1).astype(jnp.int32).astype(jnp.int16)
-
-    def from_blocks(blocks):
-        wide_blocks = blocks.astype(jnp.int32).astype(F32)
-        return wide_blocks[:, :40] * jnp.exp2(wide_blocks[:, 40:41] - 15.0)
 
     orders = (("x", "y", "z"), ("y", "z", "x"), ("z", "x", "y"))
     mine = pl.ds(core * 4, 4)
@@ -379,12 +380,6 @@
             res[f, qa, core * 4 + qb] = block
         if number < 6:
             start(number + 1, f)
-        elif f % 2 == 1:
-            c = f // 2
-            part = [from_blocks(res[f - 1 + n // 4, n % 4]).reshape(CH, 128) for n in range(8)]
-            wgo[c, 0] = jnp.concatenate([part[0], part[1], part[2][:, :64]], axis=1)
-            wgo[c, 1] = jnp.concatenate([part[2][:, 64:], part[3], part[4]], axis=1)
-            wgo[c, 2] = jnp.concatenate([part[5], part[6], part[7][:, :64]], axis=1)
 
     flows = 6
     due = sorted(
@@ -402,7 +397,7 @@
         clock[0] += us
 
     def weight_part(f):
-        c = f // 2
+        c = TAP_ROWS[f // 2]
         for n in range((f % 2) * 2, (f % 2) * 2 + 2):
             part = jnp.dot(
                 at[...],
@@ -417,6 +412,9 @@
 
     for f in range(flows):
         work(HALF_US, lambda f=f: weight_part(f))
+
+    def spread_row(k):
+        spread(a3, k, three(at[:, pl.ds((k - 1) * COLS, COLS)].astype(F32), True))
 
     def edge_a(k):
         activate(k)
@@ -522,11 +520,13 @@
     work(1.0, send_back)
     work(0.5, top_a)
     work(0.5, bottom_a)
+    for k in range(1, ROWS + 1):
+        work(0.3, lambda k=k: spread_row(k))
     for t in range(tiles):
         work(TILE_US, lambda t=t: out_tile(t))
     work(1.0, take_back)
     for row in range(ROWS):
-        work(0.4, lambda row=row: grad_row(row))
+        work(0.5, lambda row=row: grad_row(row))
     work(1.0, time_gradient)
     while due:
         event(*due.pop(0)[1:])
@@ -536,11 +536,18 @@
                 copy.wait_send()
 
 
-def store(out_v, lg_v, wg_v, tg_v, out_hbm, lg_hbm, wg_hbm, tg_hbm, sems):
-    pairs = ((wg_v, wg_hbm), (out_v, out_hbm), (lg_v, lg_hbm), (tg_v, tg_hbm))
+def store(out_v, lg_v, res, tg_v, out_hbm, lg_hbm, wg_hbm, tg_hbm, wgo, sems):
+    pairs = ((out_v, out_hbm), (lg_v, lg_hbm), (tg_v, tg_hbm))
     copies = [pltpu.make_async_copy(a, b, sems.at[n]) for n, (a, b) in enumerate(pairs)]
     for copy in copies:
         copy.start()
+    for n, c in enumerate(TAP_ROWS):
+        part = [from_blocks(res[2 * n + m // 4, m % 4]).reshape(CH, 128) for m in range(8)]
+        wgo[c, 0] = jnp.concatenate([part[0], part[1], part[2][:, :64]], axis=1)
+        wgo[c, 1] = jnp.concatenate([part[2][:, 64:], part[3], part[4]], axis=1)
+        wgo[c, 2] = jnp.concatenate([part[5], part[6], part[7][:, :64]], axis=1)
+        copies.append(pltpu.make_async_copy(wgo.at[c], wg_hbm.at[c], sems.at[3 + n]))
+        copies[-1].start()
     for copy in copies:
         copy.wait()
 
@@ -589,7 +596,6 @@
         vmem((6, 40, 128), F32),
         vmem((6, 4, 40, 128), F32),
         vmem((6, 48, 128), jnp.int16),
-        vmem((6, 4, 8, 48, 128), jnp.int16),
         vmem((3, CH, 128), F32),
         pltpu.SemaphoreType.DMA((16,)),
         pltpu.SemaphoreType.DMA((REMOTE,)),
@@ -603,7 +609,10 @@
     )
     held = pl.pallas_call(
         kernel,
-        out_shape=tuple(vmem(*shape) for shape in shapes),
+        out_shape=tuple(
+            vmem(*shape)
+            for shape in (*shapes[:2], ((6, 4, 8, 48, 128), jnp.int16), shapes[3])
+        ),
         in_specs=[anywhere] * 8,
         out_specs=[pl.BlockSpec(memory_space=pltpu.VMEM)] * 4,
         scratch_shapes=scratch,
@@ -624,10 +633,10 @@
     out, lg, wgrad, tgrad = pl.pallas_call(
         store,
         out_shape=tuple(jax.ShapeDtypeStruct(*shape) for shape in shapes),
-        in_specs=[anywhere] * 4,
+        in_specs=[anywhere, anywhere, pl.BlockSpec(memory_space=pltpu.VMEM), anywhere],
         out_specs=[anywhere] * 4,
-        scratch_shapes=[pltpu.SemaphoreType.DMA((4,))],
-        compiler_params=pltpu.CompilerParams(vmem_limit_bytes=1024 * 1024),
+        scratch_shapes=[vmem((3, 3, CH, CH), F32), pltpu.SemaphoreType.DMA((6,))],
+        compiler_params=pltpu.CompilerParams(vmem_limit_bytes=8 * 1024 * 1024),
         name="store",
     )(*held)
     out = jnp.swapaxes(out.reshape(1, ROWS, CH, COLS), 2, 3)

time: 63.5 us -> 62.2 us (0.980)
  Pallas kernels: 61.2 us -> 59.9 us
    pallas_call x1, Pallas kernels: 58.2 us -> 56.8 us  [per_device(): pl.pallas_call(kernel, out_shape=tuple((vmem(*shape) for shape in (*shape...]
where the time goes in v4:
time: 62.2 us; the launch traced here: 62.1 us
  Pallas kernels  59.9 us (96%)
  between operations  1.47 us (2%)
  other arithmetic  0.71 us (1%)
    pallas_call x1, Pallas kernels, per_device(): pl.pallas_call(kernel, out_shape=tuple((vmem(*shape) for shape in (*shape...  56.8 us
    pallas_call x1, Pallas kernels, per_device(): pl.pallas_call(store, out_shape=tuple((jax.ShapeDtypeStruct(*shape) for s...  3.12 us

profile of v4, /device:TPU:1, one launch (start us, length us, event | category | flops | bytes accessed | tf_op | source)
XLA Modules:
  0.0 62.1 jit_solution(11893745901812412675)
XLA Ops:
  1.3 0.1 sine_convert_fusion
  1.3 0.7 %maximum_convert_fusion.emb_hbm = f32[320]{0:T(512)} fusion(bf16[160]{0:T(256)(128)(2,1)S(1)} %get-tuple-element.20, bf16[160]{0:T(256)(128)(2,1)S(1)} %get-tuple-element.21), kind=kLoop, calls=%fused_computation | loop fusion | flops 1280 | bytes 1920 | tf_op jit(solution)/shard_map/convert_element_type | solution.py:624
  2.0 56.8 %block.1 = (bf16[4,320,512]{2,1,0:T(8,128)(2,1)S(1)}, bf16[4,320,512]{2,1,0:T(8,128)(2,1)S(1)}, s16[6,4,8,48,128]{4,3,2,1,0:T(8,128)(2,1)S(1)}, f32[320,320]{1,0:T(8,128)S(1)}) custom-call(f32[320]{0:T(512)} %maximum_convert_fusion.emb_hbm, bf16[4,320,512]{2,1,0:T(8,128)(2,1)} %bitcast.15, bf16[4,320,512]{2,1,0:T(8,128)(2,1)} %bitcast.16, ...), custom_call_target="tpu_custom_call" | custom-call | tf_op jit(solution)/shard_map/block/pallas_call | solution.py:610
  58.8 3.1 %store.1 = (bf16[4,320,512]{2,1,0:T(8,128)(2,1)}, bf16[4,320,512]{2,1,0:T(8,128)(2,1)}, f32[3,3,320,320]{3,2,1,0:T(8,128)}, f32[320,320]{1,0:T(8,128)}) custom-call(bf16[4,320,512]{2,1,0:T(8,128)(2,1)S(1)} %get-tuple-element.12.out_v, bf16[4,320,512]{2,1,0:T(8,128)(2,1)S(1)} %get-tuple-element.13.lg_v, s16[6,4,8,48,128]{4,3,2,1,0:T(8,128)(2,1)S(1)} %get-tuple-element.14.res, ...), custom_call_target="tpu_custom_call" | custom-call | tf_op jit(solution)/shard_map/store/pallas_call | solution.py:633

commit v5 on v4

--- a/solution.py
+++ b/solution.py
@@ -211,20 +211,17 @@
         return carry
 
     lax.fori_loop(1, ROWS + 1, spread_g, 0)
-    loads["w"].wait()
 
     def lay_out(i, carry):
         taps = wb[i].astype(F32)
         none = jnp.zeros((CH, DEEP - 3 * CH), F32)
-        wcl[:, pl.ds(pl.multiple_of(i * DEEP, DEEP), DEEP)] = jnp.concatenate(
+        wcl[:, pl.ds(i * DEEP, DEEP)] = jnp.concatenate(
             [taps.T, none], axis=1
         ).astype(BF16)
-        wgl[:, pl.ds(pl.multiple_of((2 - i) * DEEP, DEEP), DEEP)] = jnp.concatenate(
+        wgl[:, pl.ds((2 - i) * DEEP, DEEP)] = jnp.concatenate(
             [taps[0:CH], taps[CH : 2 * CH], taps[2 * CH :], none], axis=1
         ).astype(BF16)
         return carry
-
-    lax.fori_loop(0, 3, lay_out, 0)
 
     def ends_g():
         @pl.when(sp > 0)
@@ -515,6 +512,9 @@
             precision=lax.Precision.HIGHEST, preferred_element_type=F32,
         )
 
+    loads["w"].wait()
+    for i in range(3):
+        work(0.4, lambda i=i: lay_out(i, 0))
     for t in range(tiles):
         work(TILE_US, lambda t=t: back_tile(t))
     work(1.0, send_back)

time: 62.2 us -> 62.3 us (level)
  no operation moved by 1% of the time
where the time goes in v5:
time: 62.3 us; the launch traced here: 62.2 us
  Pallas kernels  60 us (96%)
  between operations  1.47 us (2%)
  other arithmetic  0.71 us (1%)
    pallas_call x1, Pallas kernels, per_device(): pl.pallas_call(kernel, out_shape=tuple((vmem(*shape) for shape in (*shape...  56.9 us
    pallas_call x1, Pallas kernels, per_device(): pl.pallas_call(store, out_shape=tuple((jax.ShapeDtypeStruct(*shape) for s...  3.12 us

profile of v5, /device:TPU:1, one launch (start us, length us, event | category | flops | bytes accessed | tf_op | source)
XLA Modules:
  0.0 62.2 jit_solution(6151397294295751118)
XLA Ops:
  1.3 0.1 sine_convert_fusion
  1.3 0.7 %maximum_convert_fusion.emb_hbm = f32[320]{0:T(512)} fusion(bf16[160]{0:T(256)(128)(2,1)S(1)} %get-tuple-element.20, bf16[160]{0:T(256)(128)(2,1)S(1)} %get-tuple-element.21), kind=kLoop, calls=%fused_computation | loop fusion | flops 1280 | bytes 1920 | tf_op jit(solution)/shard_map/convert_element_type | solution.py:624
  2.0 56.9 %block.1 = (bf16[4,320,512]{2,1,0:T(8,128)(2,1)S(1)}, bf16[4,320,512]{2,1,0:T(8,128)(2,1)S(1)}, s16[6,4,8,48,128]{4,3,2,1,0:T(8,128)(2,1)S(1)}, f32[320,320]{1,0:T(8,128)S(1)}) custom-call(f32[320]{0:T(512)} %maximum_convert_fusion.emb_hbm, bf16[4,320,512]{2,1,0:T(8,128)(2,1)} %bitcast.15, bf16[4,320,512]{2,1,0:T(8,128)(2,1)} %bitcast.16, ...), custom_call_target="tpu_custom_call" | custom-call | tf_op jit(solution)/shard_map/block/pallas_call | solution.py:610
  58.9 3.1 %store.1 = (bf16[4,320,512]{2,1,0:T(8,128)(2,1)}, bf16[4,320,512]{2,1,0:T(8,128)(2,1)}, f32[3,3,320,320]{3,2,1,0:T(8,128)}, f32[320,320]{1,0:T(8,128)}) custom-call(bf16[4,320,512]{2,1,0:T(8,128)(2,1)S(1)} %get-tuple-element.12.out_v, bf16[4,320,512]{2,1,0:T(8,128)(2,1)S(1)} %get-tuple-element.13.lg_v, s16[6,4,8,48,128]{4,3,2,1,0:T(8,128)(2,1)S(1)} %get-tuple-element.14.res, ...), custom_call_target="tpu_custom_call" | custom-call | tf_op jit(solution)/shard_map/store/pallas_call | solution.py:633
